TPU v7x, 32 devices: a whole 2x2x4 slice. The times are simulated.
32 devices in a mesh: shot: 2 (over x), gy: 16 (over z, y, core).
Axes of the slice: x: 2, y: 2, z: 4, core: 2. Of those that a mesh axis runs over, the one named last changes fastest.
Arguments:
- source_now: float32 [32, 128, 256], P('shot', 'gy'), parts along dimension 0, may hold values from -4 to 4
- source_before: float32 [32, 128, 256], P('shot', 'gy'), parts along dimension 0, may hold values from -4 to 4
- receiver_now: float32 [32, 128, 256], P('shot', 'gy'), parts along dimension 0, may hold values from -4 to 4
- receiver_before: float32 [32, 128, 256], P('shot', 'gy'), parts along dimension 0, may hold values from -4 to 4
- speed_term: float32 [16, 128, 256], P(None, 'gy'), may hold values from 0.03 to 0.12
- aniso_field: float32 [16, 128, 256], P(None, 'gy'), may hold values from 0 to 0.3
- tilt_field: float32 [16, 128, 256], P(None, 'gy'), may hold values from -0.5 to 0.5
- angle_bins: int32 [16, 128, 256], P(None, 'gy'), may hold values from 0 to 7
- weight_table: bfloat16 [24, 8, 4], replicated, may hold values from -1.25 to 1.25
- offset_lags: int32 [24], replicated, may hold values from -16 to 16, as said below
- source_cells: int32 [16], P('shot'), parts along dimension 0, may hold values from 0 to 32767
- source_wavelet: float32 [4, 8], P('shot'), parts along dimension 0, may hold values from -24 to 24
- receiver_cells: int32 [4096], P('shot'), parts along dimension 0, may hold values from 0 to 32767
- receiver_traces: float32 [4, 2048], P('shot'), parts along dimension 0, may hold values from -18 to 18
Outputs:
- angle_images: bfloat16 [8, 16, 128, 256], P('shot', None, 'gy'), parts along dimension 0
There are 2 independent parts, one for each index of `shot`. A program takes and returns all parts, laid end to end along the dimension named above; an argument that names none is the same for every part. Nothing has to cross between parts.
Inputs may be any that keep to these rules, and one draw needn't show every extreme that they name: `offset_lags`: 24 distinct lags; -16 and 16 are among them.
All inputs are finite; a program needn't handle non-finite values.
Results may differ from a plain program's by a relative error of at most 0.0051.
Values may be sent and summed in bfloat16 or wider, within the bound.
No kernel may reach another device: no remote copies, remote signals or barrier semaphores. Data moves between devices by JAX's collectives and lax.ppermute only.
A program may use at most 64 MiB of HBM per device.

v0:
```python
import functools

import jax
import jax.numpy as jnp
from jax import lax
from jax.experimental import pallas as pl
from jax.experimental.pallas import tpu as pltpu
from jax.sharding import PartitionSpec as P

STEPS = 2
SECOND = (-205.0 / 72.0, 8.0 / 5.0, -1.0 / 5.0, 8.0 / 315.0, -1.0 / 560.0)
FIRST = (4.0 / 5.0, -1.0 / 5.0, 4.0 / 105.0, -1.0 / 280.0)
REACH = 4
LANES = 128
F32 = jnp.float32
BF16 = jnp.bfloat16

VMEM = pl.BlockSpec(memory_space=pltpu.VMEM)
SMEM = pl.BlockSpec(memory_space=pltpu.SMEM)


def call(kernel, outs, in_specs, scratch, mib, flops, bytes_moved):
    multiple = isinstance(outs, (list, tuple))
    return pl.pallas_call(
        kernel,
        out_shape=outs,
        in_specs=in_specs,
        out_specs=[VMEM] * len(outs) if multiple else VMEM,
        scratch_shapes=scratch,
        compiler_params=pltpu.CompilerParams(vmem_limit_bytes=mib << 20),
        cost_estimate=pl.CostEstimate(
            flops=flops, bytes_accessed=bytes_moved, transcendentals=0
        ),
    )


def is_odd():
    return lax.axis_index("gy") % 2 == 1


def sublane(shape):
    return lax.broadcasted_iota(jnp.int32, shape, len(shape) - 2)


def pack_kernel(sn, sb, rn, rb, sp, an, ti, out_x, out_s):
    depth, rows, width = sn.shape
    half = rows // 2
    full = depth * rows
    odd = is_odd()
    for place, field in enumerate((sn, rn)):
        value = field[...].reshape(full, width).astype(BF16)
        out_x[place * full : (place + 1) * full] = value
        out_s[place * full : (place + 1) * full] = value
    first_half = sublane((depth, rows, width)) < half

    def joined(a, b, start, count):
        keep = first_half[: a.shape[0]]
        turned_a = pltpu.roll(a, half, 1)
        turned_b = pltpu.roll(b, half, 1)
        low = jnp.where(keep, a, turned_b).reshape(count, width).astype(BF16)
        high = jnp.where(keep, turned_a, b).reshape(count, width).astype(BF16)
        out_x[start : start + count] = jnp.where(odd, high, low)
        out_s[start : start + count] = jnp.where(odd, low, high)

    joined(sb[...], rb[...], 2 * full, full)
    joined(sp[...], an[...], 3 * full, full)
    joined(ti[: depth // 2], ti[depth // 2 :], 4 * full, full // 2)


def inject_kernel(grid_rows, rc, rt, sc, sw, bins, inj, bins_y, onehot, left):
    count = rc.shape[1]
    depth, rows, width = bins.shape
    first_row = lax.axis_index("gy") * rows
    half = rows // 2
    shift = width.bit_length() - 1
    power = 1 << shift == width

    def row_of(cell):
        if power:
            return lax.shift_right_logical(cell, jnp.int32(shift))
        return lax.div(cell, jnp.int32(width))

    own = lax.broadcasted_iota(jnp.int32, (rows, 1), 0)
    own_row = first_row + own
    edge = first_row + jnp.where(own < half, own + rows, own - rows)
    edge_row = jnp.where(
        edge >= grid_rows, edge - grid_rows, jnp.where(edge < 0, edge + grid_rows, edge)
    )

    for start in range(0, count, LANES):
        cells = rc[:, start : start + LANES]
        at_row = row_of(cells)
        at_col = cells - at_row * width
        cols = lax.broadcasted_iota(jnp.int32, (width, LANES), 0)
        onehot[:, start : start + LANES] = jnp.where(cols == at_col, 1.0, 0.0).astype(BF16)
        parts = []
        for step, wanted in ((0, own_row), (0, edge_row), (1, own_row)):
            amount = rt[step : step + 1, start : start + LANES]
            coarse = amount.astype(BF16).astype(F32)
            fine = amount - coarse
            here = wanted == at_row
            parts.append(jnp.where(here, coarse, 0.0))
            parts.append(jnp.where(here, fine, 0.0))
        left[:, start : start + LANES] = jnp.concatenate(parts, 0).astype(BF16)
    spread = lax.dot_general(
        left[...], onehot[...], (((1,), (1,)), ((), ())), preferred_element_type=F32
    )
    cols = lax.broadcasted_iota(jnp.int32, (rows, width), 1)
    for place, (step, wanted) in enumerate(((0, own_row), (0, edge_row), (1, own_row))):
        base = 2 * place * rows
        inj[place, 1] = spread[base : base + rows] + spread[base + rows : base + 2 * rows]
        total = jnp.zeros((rows, width), F32)
        for i in range(sc.shape[0]):
            cell = sc[i]
            at_row = lax.div(cell, jnp.int32(width))
            at_col = cell - at_row * width
            here = jnp.logical_and(wanted == at_row, cols == at_col)
            total = total + jnp.where(here, sw[step, i], 0.0)
        inj[place, 0] = total
    for y in range(rows):
        bins_y[y] = bins[:, y, :]


def shifted_x(value, k, lane):
    width = value.shape[-1]
    above = jnp.where(lane < width - k, pltpu.roll(value, width - k, 1), 0.0)
    below = jnp.where(lane >= k, pltpu.roll(value, k, 1), 0.0)
    return above, below


def flat_terms(value, y_shifts, lane):
    second = (2.0 * SECOND[0]) * value
    first = None
    for k in range(1, REACH + 1):
        above, below = shifted_x(value, k, lane)
        up, down = y_shifts[k - 1]
        second = second + SECOND[k] * ((above + below) + (up + down))
        term = FIRST[k - 1] * ((above - below) + (up - down))
        first = term if first is None else first + term
    return second, first


def depth_terms(field, slope, at):
    second = SECOND[0] * field[at + REACH]
    first = None
    for k in range(1, REACH + 1):
        second = second + SECOND[k] * (field[at + REACH + k] + field[at + REACH - k])
        term = FIRST[k - 1] * (slope[at + REACH + k] - slope[at + REACH - k])
        first = term if first is None else first + term
    return second, first


def step_kernel(
    sn, sb, rn, rb, sp, an, ti, px, ps, inj, out,
    field, slope, base, edge_sp, edge_ti, later, later_edge, turned,
):
    depth, rows, width = sn.shape
    half = rows // 2
    full = depth * rows
    odd = is_odd()
    row = sublane((rows, width))
    lane = lax.broadcasted_iota(jnp.int32, (rows, width), 1)
    low_half = row < half
    now = (sn, rn)
    before = (sb, rb)

    zeros = jnp.zeros((REACH, rows, width), F32)
    for ref in (field, slope):
        for m in range(2):
            for t in range(2):
                ref[m, t, :REACH] = zeros
                ref[m, t, REACH + depth :] = zeros
    for m in range(2):
        later[m, :REACH] = zeros
        later[m, REACH + depth :] = zeros

    def from_packs(start):
        x = px[pl.ds(start, 2 * rows), :].astype(F32)
        s = ps[pl.ds(start, 2 * rows), :].astype(F32)
        return jnp.where(odd, s, x), jnp.where(odd, x, s)

    def roll(value, k):
        return pltpu.roll(value, k % rows, 0)

    def edge_pair(low, high):
        first = jnp.where(low_half, high, roll(low, half))
        second = jnp.where(low_half, roll(high, half), low)
        return first, second

    def tilt_edge(pair, c):
        start = pl.multiple_of(4 * full + pair * 2 * rows, 2 * rows)
        low2, high2 = from_packs(start)
        for j in range(2):
            part = slice(j * rows, (j + 1) * rows)
            a, b = edge_pair(low2[part], high2[part])
            edge_ti[2 * pair + j] = a
            edge_ti[2 * pair + j + depth // 2] = b
        return c

    lax.fori_loop(0, depth // 4, tilt_edge, 0, unroll=2)

    def flat(pair, c):
        offset = pair * 2 * rows
        starts = [pl.multiple_of(n * full + offset, 2 * rows) for n in range(4)]
        current = [from_packs(starts[m]) for m in range(2)]
        old_low, old_high = from_packs(starts[2])
        media_low, media_high = from_packs(starts[3])
        for j in range(2):
            part = slice(j * rows, (j + 1) * rows)
            z = 2 * pair + j
            old = edge_pair(old_low[part], old_high[part])
            speed_edge, aniso_edge = edge_pair(media_low[part], media_high[part])
            edge_sp[z] = speed_edge
            factor = (sp[z] * (1.0 + 2.0 * an[z]), speed_edge * (1.0 + 2.0 * aniso_edge))
            for m in range(2):
                low, high = current[m][0][part], current[m][1][part]
                mid = now[m][z]
                edge = jnp.where(low_half, high, low)
                own_shifts, edge_shifts = [], []
                for k in range(1, REACH + 1):
                    mid_up, mid_down = roll(mid, -k), roll(mid, k)
                    low_up, low_down = roll(low, -k), roll(low, k)
                    high_up, high_down = roll(high, -k), roll(high, k)
                    own_shifts.append(
                        (
                            jnp.where(row < rows - k, mid_up, high_up),
                            jnp.where(row >= k, mid_down, low_down),
                        )
                    )
                    edge_shifts.append(
                        (
                            jnp.where(
                                low_half, high_up, jnp.where(row < rows - k, low_up, mid_up)
                            ),
                            jnp.where(
                                low_half, jnp.where(row >= k, high_down, mid_down), low_down
                            ),
                        )
                    )
                for t, (value, shifts, prior) in enumerate(
                    ((mid, own_shifts, before[m][z]), (edge, edge_shifts, old[m]))
                ):
                    second, first = flat_terms(value, shifts, lane)
                    field[m, t, z + REACH] = value
                    slope[m, t, z + REACH] = first
                    base[m, t, z] = 2.0 * value - prior + factor[t] * second
        return c

    lax.fori_loop(0, depth // 2, flat, 0)

    def deep(z, c):
        speed = (sp[z], edge_sp[z])
        tilt = (ti[z], edge_ti[z])
        for m in range(2):
            for t in range(2):
                second, first = depth_terms(field.at[m, t], slope.at[m, t], z)
                value = base[m, t, z] + speed[t] * (second + tilt[t] * first)
                if t == 0:
                    later[m, z + REACH] = value
                else:
                    later_edge[m, z] = value
        return c

    lax.fori_loop(0, depth, deep, 0, unroll=2)
    for m in range(2):
        later[m, REACH] = later[m, REACH] + inj[0, m]
        later_edge[m, 0] = later_edge[m, 0] + inj[1, m]

    def flat_later(z, c):
        factor = sp[z] * (1.0 + 2.0 * an[z])
        for m in range(2):
            mid = later[m, z + REACH]
            edge = later_edge[m, z]
            shifts = []
            for k in range(1, REACH + 1):
                shifts.append(
                    (
                        jnp.where(row < rows - k, roll(mid, -k), roll(edge, -k)),
                        jnp.where(row >= k, roll(mid, k), roll(edge, k)),
                    )
                )
            second, first = flat_terms(mid, shifts, lane)
            slope[m, 0, z + REACH] = first
            base[m, 0, z] = 2.0 * mid - now[m][z] + factor * second
            for part in range(width // LANES):
                turned[0, m, part, pl.ds(z, rows, stride=depth), :] = mid[
                    :, part * LANES : (part + 1) * LANES
                ]
        return c

    lax.fori_loop(0, depth, flat_later, 0, unroll=2)

    def deep_later(z, c):
        surface = jnp.where(z == 0, 1.0, 0.0)
        for m in range(2):
            second, first = depth_terms(later.at[m], slope.at[m, 0], z)
            value = base[m, 0, z] + sp[z] * (second + ti[z] * first) + surface * inj[2, m]
            for part in range(width // LANES):
                turned[1, m, part, pl.ds(z, rows, stride=depth), :] = value[
                    :, part * LANES : (part + 1) * LANES
                ]
        return c

    lax.fori_loop(0, depth, deep_later, 0, unroll=2)
    for s in range(STEPS):
        for m in range(2):
            for part in range(width // LANES):
                for y in range(rows):
                    out[s, m, y, :, part * LANES : (part + 1) * LANES] = turned[
                        s, m, part, y * depth : (y + 1) * depth, :
                    ].astype(BF16)


def image_kernel(lags, far, near, own, chip, relay, bins, table, out, window, turned):
    rows, depth, width = bins.shape
    lag_count, angles = table.shape[:2]
    odd = jnp.where(is_odd(), 1, 0)
    for piece, place in ((far, 0), (near, 1), (own, 2), (chip, 3), (relay, 4)):
        block = (place + odd * (4 - 2 * place)) * rows
        for s in range(STEPS):
            for m in range(2):
                window[s, m, pl.ds(block, rows)] = piece[s, m].astype(F32)
    tiles = [(z, x) for z in range(0, depth, 8) for x in range(0, width, LANES)]

    def one_row(y, c):
        ids = bins[y]

        def one_lag(h, sums):
            lag = lags[h]
            at_s = y + 2 * rows - lag
            at_r = y + 2 * rows + lag
            sums = [list(a) for a in sums]
            for n, (z, x) in enumerate(tiles):
                zs, xs = slice(z, z + 8), slice(x, x + LANES)
                product = window[0, 0, at_s, zs, xs] * window[0, 1, at_r, zs, xs]
                for s in range(1, STEPS):
                    product = product + window[s, 0, at_s, zs, xs] * window[s, 1, at_r, zs, xs]
                for a in range(angles):
                    weight = jnp.take_along_axis(table[h, a], ids[zs, xs], axis=0)
                    sums[a][n] = sums[a][n] + weight * product
            return tuple(tuple(a) for a in sums)

        zero = jnp.zeros((8, LANES), F32)
        sums = lax.fori_loop(
            0, lag_count, one_lag, tuple((zero,) * len(tiles) for _ in range(angles)), unroll=4
        )
        for a in range(angles):
            for n, (z, x) in enumerate(tiles):
                turned[a, x // LANES, pl.ds(z * rows + y, 8, stride=rows), :] = sums[a][n]
        return c

    lax.fori_loop(0, rows, one_row, 0)
    for a in range(angles):
        for part in range(width // LANES):
            out[a, :, :, part * LANES : (part + 1) * LANES] = (
                turned[a, part].astype(BF16).reshape(depth, rows, LANES)
            )


def per_device(
    source_now, source_before, receiver_now, receiver_before, speed_term, aniso_field,
    tilt_field, angle_bins, weight_table, offset_lags, source_cells, source_wavelet,
    receiver_cells, receiver_traces,
):
    depth, rows, width = source_now.shape
    size = lax.axis_size("gy")
    full = depth * rows
    lag_count, bin_count, angles = weight_table.shape
    count = receiver_cells.shape[0]
    parts = width // LANES

    chip_route = [(i, i ^ 1) for i in range(size)]
    near_route = [(i, (i + 1 if i % 2 else i - 1) % size) for i in range(size)]
    far_route = [(i, (i - 2 if i % 2 else i + 2) % size) for i in range(size)]

    def moved(block, route):
        return lax.ppermute(block, "gy", route)

    fields = (
        source_now, source_before, receiver_now, receiver_before, speed_term, aniso_field,
        tilt_field,
    )
    pack_shape = jax.ShapeDtypeStruct((4 * full + full // 2, width), BF16)
    pack_x, pack_s = call(
        pack_kernel, [pack_shape] * 2, [VMEM] * 7, [], 8, full * width * 20, full * width * 40
    )(*fields)
    got_s = moved(pack_s, chip_route)
    got_x = moved(pack_x, near_route)

    inj, bins_y = call(
        functools.partial(inject_kernel, size * rows),
        [
            jax.ShapeDtypeStruct((3, 2, rows, width), F32),
            jax.ShapeDtypeStruct((rows, depth, width), jnp.int32),
        ],
        [VMEM, VMEM, SMEM, SMEM, VMEM],
        [pltpu.VMEM((width, count), BF16), pltpu.VMEM((6 * rows, count), BF16)],
        8,
        12 * rows * count * width,
        full * width * 8,
    )(receiver_cells[None], receiver_traces, source_cells, source_wavelet, angle_bins)
    table = jnp.broadcast_to(
        jnp.transpose(weight_table, (0, 2, 1)).astype(F32)[..., None],
        (lag_count, angles, bin_count, LANES),
    )

    padded = (2, 2, depth + 2 * REACH, rows, width)
    own = call(
        step_kernel,
        jax.ShapeDtypeStruct((STEPS, 2, rows, depth, width), BF16),
        [VMEM] * 10,
        [
            pltpu.VMEM(padded, F32),
            pltpu.VMEM(padded, F32),
            pltpu.VMEM((2, 2, depth, rows, width), F32),
            pltpu.VMEM((depth, rows, width), F32),
            pltpu.VMEM((depth, rows, width), F32),
            pltpu.VMEM((2, depth + 2 * REACH, rows, width), F32),
            pltpu.VMEM((2, depth, rows, width), F32),
            pltpu.VMEM((STEPS, 2, parts, full, LANES), F32),
        ],
        16,
        full * width * 600,
        full * width * 50,
    )(*fields, got_x, got_s, inj)

    far = moved(own, far_route)
    near = moved(own, near_route)
    chip = moved(own, chip_route)
    relay = moved(near, chip_route)
    return call(
        image_kernel,
        jax.ShapeDtypeStruct((angles, depth, rows, width), BF16),
        [SMEM] + [VMEM] * 7,
        [
            pltpu.VMEM((STEPS, 2, 5 * rows, depth, width), F32),
            pltpu.VMEM((angles, parts, full, LANES), F32),
        ],
        16,
        full * width * 24 * 12,
        full * width * 20,
    )(offset_lags, far, near, own, chip, relay, bins_y, table)


def solution(mesh):
    grid = P("shot", "gy", None)
    media = P(None, "gy", None)
    return jax.shard_map(
        per_device,
        mesh=mesh,
        in_specs=(grid,) * 4
        + (media,) * 4
        + (P(), P(), P("shot"), P("shot", None), P("shot"), P("shot", None)),
        out_specs=P("shot", None, "gy", None),
        check_vma=False,
    )
```

profile of v0, /device:TPU:29, one launch (start us, length us, event | category | flops | bytes accessed | tf_op | source)
XLA Modules:
  0.0 39.7 jit_solution(13818078853055693308)
XLA Ops:
  0.0 0.0 copy-start
  0.0 0.9 %copy-done = f32[16,8,256]{2,1,0:T(8,128)S(1)} copy-done((f32[16,8,256]{2,1,0:T(8,128)S(1)}, f32[16,8,256]{2,1,0:T(8,128)}, u32[]{:S(2)}) %copy-start) | copy-done | bytes 131096
  0.9 0.0 copy-start.2
  0.9 0.9 %copy-done.2 = f32[16,8,256]{2,1,0:T(8,128)S(1)} copy-done((f32[16,8,256]{2,1,0:T(8,128)S(1)}, f32[16,8,256]{2,1,0:T(8,128)}, u32[]{:S(2)}) %copy-start.2) | copy-done | bytes 131096
  1.8 0.0 copy-start.4
  1.8 0.9 %copy-done.4 = f32[16,8,256]{2,1,0:T(8,128)S(1)} copy-done((f32[16,8,256]{2,1,0:T(8,128)S(1)}, f32[16,8,256]{2,1,0:T(8,128)}, u32[]{:S(2)}) %copy-start.4) | copy-done | bytes 131096
  2.7 0.0 copy-start.6
  2.7 0.9 %copy-done.6 = f32[16,8,256]{2,1,0:T(8,128)S(1)} copy-done((f32[16,8,256]{2,1,0:T(8,128)S(1)}, f32[16,8,256]{2,1,0:T(8,128)}, u32[]{:S(2)}) %copy-start.6) | copy-done | bytes 131096
  3.6 0.0 copy-start.8
  3.6 0.9 %copy-done.8 = f32[16,8,256]{2,1,0:T(8,128)S(1)} copy-done((f32[16,8,256]{2,1,0:T(8,128)S(1)}, f32[16,8,256]{2,1,0:T(8,128)}, u32[]{:S(2)}) %copy-start.8) | copy-done | bytes 131096
  4.5 0.0 copy-start.10
  4.5 0.9 %copy-done.10 = f32[16,8,256]{2,1,0:T(8,128)S(1)} copy-done((f32[16,8,256]{2,1,0:T(8,128)S(1)}, f32[16,8,256]{2,1,0:T(8,128)}, u32[]{:S(2)}) %copy-start.10) | copy-done | bytes 131096
  5.4 0.0 copy-start.12
  5.4 0.9 %copy-done.12 = f32[16,8,256]{2,1,0:T(8,128)S(1)} copy-done((f32[16,8,256]{2,1,0:T(8,128)S(1)}, f32[16,8,256]{2,1,0:T(8,128)}, u32[]{:S(2)}) %copy-start.12) | copy-done | bytes 131096
  6.3 0.0 copy-start.15
  6.3 0.0 copy-start.3
  6.3 0.0 copy-start.5
  6.3 0.0 copy-start.7
  6.3 0.0 copy-start.9
  6.4 0.0 copy-start.11
  6.4 0.0 copy-start.13
  6.4 0.1 shard_map.136
  6.5 0.0 copy-start.1
  6.5 0.1 collective-permute-start
  6.6 0.7 %collective-permute-start.1 = (bf16[576,256]{1,0:T(8,128)(2,1)S(1)}, bf16[576,256]{1,0:T(8,128)(2,1)S(1)}, u32[]{:S(2)}, u32[]{:S(2)}) collective-permute-start(bf16[576,256]{1,0:T(8,128)(2,1)S(1)} %get-tuple-element.10), channel_id=1, source_target_pairs={{0,1},{1,0},{2,3},{3,2},{4,5},{5,4},{6,7},{7,6},{8,9},{9,8},{10,11... | collective-permute-start | bytes 884744 | tf_op jit(solution)/shard_map/ppermute | solution.py:377
  7.3 0.0 copy-done.15
  7.3 0.0 copy-start.16
  7.3 0.7 %copy-done.16 = f32[2,2048]{1,0:T(2,128)S(1)} copy-done((f32[2,2048]{1,0:T(2,128)S(1)}, f32[2,2048]{1,0:T(2,128)}, u32[]{:S(2)}) %copy-start.16) | copy-done | bytes 16408
  8.0 0.0 copy-start.17
  8.0 0.7 %copy-done.17 = s32[2048]{0:T(1024)S(1)} copy-done((s32[2048]{0:T(1024)S(1)}, s32[2048]{0:T(1024)}, u32[]{:S(2)}) %copy-start.17) | copy-done | bytes 8216
  8.7 0.0 copy-start.18
  8.7 0.7 %copy-done.18 = f32[2,8]{1,0:T(2,128)S(1)} copy-done((f32[2,8]{1,0:T(2,128)S(1)}, f32[2,8]{1,0:T(2,128)}, u32[]{:S(2)}) %copy-start.18) | copy-done | bytes 88
  9.4 0.0 copy-start.19
  9.4 0.7 %copy-done.19 = s32[8]{0:T(128)S(1)} copy-done((s32[8]{0:T(128)S(1)}, s32[8]{0:T(128)}, u32[]{:S(2)}) %copy-start.19) | copy-done | bytes 56
  10.1 1.2 %shard_map.137 = (f32[3,2,8,256]{3,2,1,0:T(8,128)S(1)}, s32[8,16,256]{2,1,0:T(8,128)S(1)}) custom-call(s32[1,2048]{1,0:T(1,128)S(1)} %bitcast.3, f32[2,2048]{1,0:T(2,128)S(1)} %copy-done.16, s32[8]{0:T(128)S(1)} %copy-done.19, f32[2,8]{1,0:T(2,128)S(1)} %copy-done.18, s32[16,8,256]{2,1,0:T(8,128)S(1)} %copy-done.15), custom_call_target="tpu_custom_call" | custom-call | flops 50331648 | bytes 262144 | tf_op jit(solution)/shard_map/pallas_call | solution.py:390
  11.3 4.2 %collective-permute-done.px = bf16[576,256]{1,0:T(8,128)(2,1)S(1)} collective-permute-done((bf16[576,256]{1,0:T(8,128)(2,1)S(1)}, bf16[576,256]{1,0:T(8,128)(2,1)S(1)}, u32[]{:S(2)}, u32[]{:S(2)}) %collective-permute-start) | collective-permute-done | bytes 294944 | tf_op jit(solution)/shard_map/ppermute | solution.py:377
  15.5 0.0 collective-permute-done.1.ps
  15.5 0.0 copy-done.3
  15.5 0.0 copy-done.5
  15.5 0.0 copy-done.7
  15.5 0.0 copy-done.9
  15.5 0.0 copy-done.11
  15.5 0.0 copy-done.13
  15.6 0.0 copy-done.1
  15.6 0.0 copy-start.20
  15.6 4.1 %shard_map.138.own = bf16[2,2,8,16,256]{4,3,2,1,0:T(8,128)(2,1)S(1)} custom-call(f32[16,8,256]{2,1,0:T(8,128)S(1)} %copy-done.1, f32[16,8,256]{2,1,0:T(8,128)S(1)} %copy-done.3, f32[16,8,256]{2,1,0:T(8,128)S(1)} %copy-done.5, f32[16,8,256]{2,1,0:T(8,128)S(1)} %copy-done.7, f32[16,8,256]{2,1,0:T(8,128)S(1)} %copy-done.9, f32[16,8,256]{2,1,0:T(8,128)S(1)} %copy-done.11, ...), custom_call_target="tpu_custom_call" | custom-call | flops 19660800 | bytes 1638400 | tf_op jit(solution)/shard_map/pallas_call | solution.py:408
  19.7 0.1 collective-permute-start.3
  19.8 1.1 %collective-permute-start.4 = (bf16[2,2,8,16,256]{4,3,2,1,0:T(8,128)(2,1)S(1)}, bf16[2,2,8,16,256]{4,3,2,1,0:T(8,128)(2,1)S(1)}, u32[]{:S(2)}, u32[]{:S(2)}) collective-permute-start(bf16[2,2,8,16,256]{4,3,2,1,0:T(8,128)(2,1)S(1)} %shard_map.138.own), channel_id=1, source_target_pairs={{0,1},{1,0},{2,3},{3,2},{4,5},{5,4},{6,7},{7,6},{8,9},{9,8},{10,11... | collective-permute-start | bytes 786440 | tf_op jit(solution)/shard_map/ppermute | solution.py:377
  20.9 1.3 %collective-permute-start.2 = (bf16[2,2,8,16,256]{4,3,2,1,0:T(8,128)(2,1)S(1)}, bf16[2,2,8,16,256]{4,3,2,1,0:T(8,128)(2,1)S(1)}, u32[]{:S(2)}, u32[]{:S(2)}) collective-permute-start(bf16[2,2,8,16,256]{4,3,2,1,0:T(8,128)(2,1)S(1)} %shard_map.138.own), channel_id=1, source_target_pairs={{0,2},{1,15},{2,4},{3,1},{4,6},{5,3},{6,8},{7,5},{8,10},{9,7},{10,... | collective-permute-start | bytes 786440 | tf_op jit(solution)/shard_map/ppermute | solution.py:377
  22.2 8.5 %collective-permute-done.3.near = bf16[2,2,8,16,256]{4,3,2,1,0:T(8,128)(2,1)S(1)} collective-permute-done((bf16[2,2,8,16,256]{4,3,2,1,0:T(8,128)(2,1)S(1)}, bf16[2,2,8,16,256]{4,3,2,1,0:T(8,128)(2,1)S(1)}, u32[]{:S(2)}, u32[]{:S(2)}) %collective-permute-start.3) | collective-permute-done | bytes 262176 | tf_op jit(solution)/shard_map/ppermute | solution.py:377
  30.6 3.7 %collective-permute-start.5 = (bf16[2,2,8,16,256]{4,3,2,1,0:T(8,128)(2,1)S(1)}, bf16[2,2,8,16,256]{4,3,2,1,0:T(8,128)(2,1)S(1)}, u32[]{:S(2)}, u32[]{:S(2)}) collective-permute-start(bf16[2,2,8,16,256]{4,3,2,1,0:T(8,128)(2,1)S(1)} %collective-permute-done.3.near), channel_id=1, source_target_pairs={{0,1},{1,0},{2,3},{3,2},{4,5},{5,4},{6,7},{7,6},{8,9},{9,8},{10,11... | collective-permute-start | bytes 786440 | tf_op jit(solution)/shard_map/ppermute | solution.py:377
  34.3 0.0 copy-done.20
  34.3 0.1 copy.15
  34.4 0.0 collective-permute-done.4.chip
  34.4 0.0 collective-permute-done.2.far
  34.4 1.0 %collective-permute-done.5.relay = bf16[2,2,8,16,256]{4,3,2,1,0:T(8,128)(2,1)S(1)} collective-permute-done((bf16[2,2,8,16,256]{4,3,2,1,0:T(8,128)(2,1)S(1)}, bf16[2,2,8,16,256]{4,3,2,1,0:T(8,128)(2,1)S(1)}, u32[]{:S(2)}, u32[]{:S(2)}) %collective-permute-start.5) | collective-permute-done | bytes 262176 | tf_op jit(solution)/shard_map/ppermute | solution.py:377
  35.5 0.0 copy-start.14
  35.5 0.2 broadcast_in_dim.10.table
  35.6 0.5 %copy-done.14 = s32[24]{0:T(128)S(1)} copy-done((s32[24]{0:T(128)S(1)}, s32[24]{0:T(128)}, u32[]{:S(2)}) %copy-start.14) | copy-done | bytes 120
  36.1 3.6 %shard_map.139 = bf16[4,16,8,256]{3,2,1,0:T(8,128)(2,1)} custom-call(s32[24]{0:T(128)S(1)} %copy-done.14, bf16[2,2,8,16,256]{4,3,2,1,0:T(8,128)(2,1)S(1)} %collective-permute-done.2.far, bf16[2,2,8,16,256]{4,3,2,1,0:T(8,128)(2,1)S(1)} %collective-permute-done.3.near, bf16[2,2,8,16,256]{4,3,2,1,0:T(8,128)(2,1)S(1)} %shard_map.138.own, ...), custom_call_target="tpu_custom_call" | custom-call | flops 9437184 | bytes 655360 | tf_op jit(solution)/shard_map/pallas_call | solution.py:431
  (1 shorter events, 0.0 us)
Async XLA Ops:
  0.0 0.9 %copy-start = (f32[16,8,256]{2,1,0:T(8,128)S(1)}, f32[16,8,256]{2,1,0:T(8,128)}, u32[]{:S(2)}) copy-start(f32[16,8,256]{2,1,0:T(8,128)} %sn.3) | copy-start | bytes 393220
  0.9 0.9 %copy-start.2 = (f32[16,8,256]{2,1,0:T(8,128)S(1)}, f32[16,8,256]{2,1,0:T(8,128)}, u32[]{:S(2)}) copy-start(f32[16,8,256]{2,1,0:T(8,128)} %sb.3) | copy-start | bytes 393220
  1.8 0.9 %copy-start.4 = (f32[16,8,256]{2,1,0:T(8,128)S(1)}, f32[16,8,256]{2,1,0:T(8,128)}, u32[]{:S(2)}) copy-start(f32[16,8,256]{2,1,0:T(8,128)} %rn.3) | copy-start | bytes 393220
  2.7 0.9 %copy-start.6 = (f32[16,8,256]{2,1,0:T(8,128)S(1)}, f32[16,8,256]{2,1,0:T(8,128)}, u32[]{:S(2)}) copy-start(f32[16,8,256]{2,1,0:T(8,128)} %rb.3) | copy-start | bytes 393220
  3.6 0.9 %copy-start.8 = (f32[16,8,256]{2,1,0:T(8,128)S(1)}, f32[16,8,256]{2,1,0:T(8,128)}, u32[]{:S(2)}) copy-start(f32[16,8,256]{2,1,0:T(8,128)} %sp.3) | copy-start | bytes 393220
  4.5 0.9 %copy-start.10 = (f32[16,8,256]{2,1,0:T(8,128)S(1)}, f32[16,8,256]{2,1,0:T(8,128)}, u32[]{:S(2)}) copy-start(f32[16,8,256]{2,1,0:T(8,128)} %an.3) | copy-start | bytes 393220
  5.4 0.9 %copy-start.12 = (f32[16,8,256]{2,1,0:T(8,128)S(1)}, f32[16,8,256]{2,1,0:T(8,128)}, u32[]{:S(2)}) copy-start(f32[16,8,256]{2,1,0:T(8,128)} %ti.3) | copy-start | bytes 393220
  6.3 1.0 %copy-start.15 = (s32[16,8,256]{2,1,0:T(8,128)S(1)}, s32[16,8,256]{2,1,0:T(8,128)}, u32[]{:S(2)}) copy-start(s32[16,8,256]{2,1,0:T(8,128)} %bins.1) | copy-start | bytes 393220
  6.3 9.2 %copy-start.3 = (f32[16,8,256]{2,1,0:T(8,128)S(1)}, f32[16,8,256]{2,1,0:T(8,128)}, u32[]{:S(2)}) copy-start(f32[16,8,256]{2,1,0:T(8,128)} %sb.3) | copy-start | bytes 393220
  6.3 9.2 %copy-start.5 = (f32[16,8,256]{2,1,0:T(8,128)S(1)}, f32[16,8,256]{2,1,0:T(8,128)}, u32[]{:S(2)}) copy-start(f32[16,8,256]{2,1,0:T(8,128)} %rn.3) | copy-start | bytes 393220
  6.3 9.2 %copy-start.7 = (f32[16,8,256]{2,1,0:T(8,128)S(1)}, f32[16,8,256]{2,1,0:T(8,128)}, u32[]{:S(2)}) copy-start(f32[16,8,256]{2,1,0:T(8,128)} %rb.3) | copy-start | bytes 393220
  6.3 9.2 %copy-start.9 = (f32[16,8,256]{2,1,0:T(8,128)S(1)}, f32[16,8,256]{2,1,0:T(8,128)}, u32[]{:S(2)}) copy-start(f32[16,8,256]{2,1,0:T(8,128)} %sp.3) | copy-start | bytes 393220
  6.4 9.2 %copy-start.11 = (f32[16,8,256]{2,1,0:T(8,128)S(1)}, f32[16,8,256]{2,1,0:T(8,128)}, u32[]{:S(2)}) copy-start(f32[16,8,256]{2,1,0:T(8,128)} %an.3) | copy-start | bytes 393220
  6.4 9.2 %copy-start.13 = (f32[16,8,256]{2,1,0:T(8,128)S(1)}, f32[16,8,256]{2,1,0:T(8,128)}, u32[]{:S(2)}) copy-start(f32[16,8,256]{2,1,0:T(8,128)} %ti.3) | copy-start | bytes 393220
  6.5 9.1 %copy-start.1 = (f32[16,8,256]{2,1,0:T(8,128)S(1)}, f32[16,8,256]{2,1,0:T(8,128)}, u32[]{:S(2)}) copy-start(f32[16,8,256]{2,1,0:T(8,128)} %sn.3) | copy-start | bytes 393220
  6.5 9.0 %collective-permute-start = (bf16[576,256]{1,0:T(8,128)(2,1)S(1)}, bf16[576,256]{1,0:T(8,128)(2,1)S(1)}, u32[]{:S(2)}, u32[]{:S(2)}) collective-permute-start(bf16[576,256]{1,0:T(8,128)(2,1)S(1)} %get-tuple-element.9), channel_id=1, source_target_pairs={{0,15},{1,2},{2,1},{3,4},{4,3},{5,6},{6,5},{7,8},{8,7},{9,10},{10,... | collective-permute-start | bytes 884744 | tf_op jit(solution)/shard_map/ppermute | solution.py:377
  6.6 8.9 %collective-permute-start.1 = (bf16[576,256]{1,0:T(8,128)(2,1)S(1)}, bf16[576,256]{1,0:T(8,128)(2,1)S(1)}, u32[]{:S(2)}, u32[]{:S(2)}) collective-permute-start(bf16[576,256]{1,0:T(8,128)(2,1)S(1)} %get-tuple-element.10), channel_id=1, source_target_pairs={{0,1},{1,0},{2,3},{3,2},{4,5},{5,4},{6,7},{7,6},{8,9},{9,8},{10,11... | collective-permute-start | bytes 884744 | tf_op jit(solution)/shard_map/ppermute | solution.py:377
  7.3 0.7 %copy-start.16 = (f32[2,2048]{1,0:T(2,128)S(1)}, f32[2,2048]{1,0:T(2,128)}, u32[]{:S(2)}) copy-start(f32[2,2048]{1,0:T(2,128)} %rt.1) | copy-start | bytes 49156
  8.0 0.7 %copy-start.17 = (s32[2048]{0:T(1024)S(1)}, s32[2048]{0:T(1024)}, u32[]{:S(2)}) copy-start(s32[2048]{0:T(1024)} %param.26) | copy-start | bytes 24580
  8.7 0.7 %copy-start.18 = (f32[2,8]{1,0:T(2,128)S(1)}, f32[2,8]{1,0:T(2,128)}, u32[]{:S(2)}) copy-start(f32[2,8]{1,0:T(2,128)} %sw.1) | copy-start | bytes 196
  9.4 0.7 %copy-start.19 = (s32[8]{0:T(128)S(1)}, s32[8]{0:T(128)}, u32[]{:S(2)}) copy-start(s32[8]{0:T(128)} %sc.1) | copy-start | bytes 100
  15.6 18.7 %copy-start.20 = (bf16[24,8,4]{0,2,1:T(4,128)(2,1)S(1)}, bf16[24,8,4]{0,2,1:T(4,128)(2,1)}, u32[]{:S(2)}) copy-start(bf16[24,8,4]{0,2,1:T(4,128)(2,1)} %param.22) | copy-start | bytes 4612
  19.7 10.9 %collective-permute-start.3 = (bf16[2,2,8,16,256]{4,3,2,1,0:T(8,128)(2,1)S(1)}, bf16[2,2,8,16,256]{4,3,2,1,0:T(8,128)(2,1)S(1)}, u32[]{:S(2)}, u32[]{:S(2)}) collective-permute-start(bf16[2,2,8,16,256]{4,3,2,1,0:T(8,128)(2,1)S(1)} %shard_map.138.own), channel_id=1, source_target_pairs={{0,15},{1,2},{2,1},{3,4},{4,3},{5,6},{6,5},{7,8},{8,7},{9,10},{10,... | collective-permute-start | bytes 786440 | tf_op jit(solution)/shard_map/ppermute | solution.py:377
  19.8 14.6 %collective-permute-start.4 = (bf16[2,2,8,16,256]{4,3,2,1,0:T(8,128)(2,1)S(1)}, bf16[2,2,8,16,256]{4,3,2,1,0:T(8,128)(2,1)S(1)}, u32[]{:S(2)}, u32[]{:S(2)}) collective-permute-start(bf16[2,2,8,16,256]{4,3,2,1,0:T(8,128)(2,1)S(1)} %shard_map.138.own), channel_id=1, source_target_pairs={{0,1},{1,0},{2,3},{3,2},{4,5},{5,4},{6,7},{7,6},{8,9},{9,8},{10,11... | collective-permute-start | bytes 786440 | tf_op jit(solution)/shard_map/ppermute | solution.py:377
  20.9 13.5 %collective-permute-start.2 = (bf16[2,2,8,16,256]{4,3,2,1,0:T(8,128)(2,1)S(1)}, bf16[2,2,8,16,256]{4,3,2,1,0:T(8,128)(2,1)S(1)}, u32[]{:S(2)}, u32[]{:S(2)}) collective-permute-start(bf16[2,2,8,16,256]{4,3,2,1,0:T(8,128)(2,1)S(1)} %shard_map.138.own), channel_id=1, source_target_pairs={{0,2},{1,15},{2,4},{3,1},{4,6},{5,3},{6,8},{7,5},{8,10},{9,7},{10,... | collective-permute-start | bytes 786440 | tf_op jit(solution)/shard_map/ppermute | solution.py:377
  30.6 4.8 %collective-permute-start.5 = (bf16[2,2,8,16,256]{4,3,2,1,0:T(8,128)(2,1)S(1)}, bf16[2,2,8,16,256]{4,3,2,1,0:T(8,128)(2,1)S(1)}, u32[]{:S(2)}, u32[]{:S(2)}) collective-permute-start(bf16[2,2,8,16,256]{4,3,2,1,0:T(8,128)(2,1)S(1)} %collective-permute-done.3.near), channel_id=1, source_target_pairs={{0,1},{1,0},{2,3},{3,2},{4,5},{5,4},{6,7},{7,6},{8,9},{9,8},{10,11... | collective-permute-start | bytes 786440 | tf_op jit(solution)/shard_map/ppermute | solution.py:377
  35.5 0.7 %copy-start.14 = (s32[24]{0:T(128)S(1)}, s32[24]{0:T(128)}, u32[]{:S(2)}) copy-start(s32[24]{0:T(128)} %lags.1) | copy-start | bytes 292
where the time goes:
time: 40.1 us; the launch traced here: 39.7 us
  waiting for transfers between devices  13.8 us (34%)
  local copies, waits for them, and re-layouts  9.85 us (25%)
  Pallas kernels  8.99 us (22%)
  starting transfers between devices  6.93 us (17%)
    ppermute x6, waiting for transfers between devices, moved(): return lax.ppermute(block, 'gy', route)  13.8 us
    unnamed x42, local copies, waits for them, and re-layouts  9.61 us
    ppermute x6, starting transfers between devices, moved(): return lax.ppermute(block, 'gy', route)  6.93 us
    pallas_call x1, Pallas kernels, per_device(): call(step_kernel, jax.ShapeDtypeStruct((STEPS, 2, rows, depth, width), BF...  4.12 us
    pallas_call x1, Pallas kernels, per_device(): call(image_kernel, jax.ShapeDtypeStruct((angles, depth, rows, width), BF1...  3.59 us
    pallas_call x1, Pallas kernels, per_device(): call(functools.partial(inject_kernel, size * rows), [jax.ShapeDtypeStruct...  1.18 us
  transfers between devices with their start and end apart: 6, of which 3 were waited for; matrix products, arithmetic and copies ran while one was open for 0% of the time, Pallas kernels for 3%

commit v1 on v0

--- a/solution.py
+++ b/solution.py
@@ -6,6 +6,7 @@
 from jax.experimental import pallas as pl
 from jax.experimental.pallas import tpu as pltpu
 from jax.sharding import PartitionSpec as P
+
 
 STEPS = 2
 SECOND = (-205.0 / 72.0, 8.0 / 5.0, -1.0 / 5.0, 8.0 / 315.0, -1.0 / 560.0)
@@ -16,7 +17,21 @@
 BF16 = jnp.bfloat16
 
 VMEM = pl.BlockSpec(memory_space=pltpu.VMEM)
-SMEM = pl.BlockSpec(memory_space=pltpu.SMEM)
+HBM = pl.BlockSpec(memory_space=pltpu.HBM)
+
+
+def in_hbm(arrays):
+    return [pltpu.with_memory_space_constraint(array, pltpu.HBM) for array in arrays]
+
+
+def fetch(sources, targets, sems):
+    copies = [
+        pltpu.make_async_copy(source, target, sems.at[n])
+        for n, (source, target) in enumerate(zip(sources, targets))
+    ]
+    for copy in copies:
+        copy.start()
+    return copies
 
 
 def call(kernel, outs, in_specs, scratch, mib, flops, bytes_moved):
@@ -42,12 +57,17 @@
     return lax.broadcasted_iota(jnp.int32, shape, len(shape) - 2)
 
 
-def pack_kernel(sn, sb, rn, rb, sp, an, ti, out_x, out_s):
+def pack_kernel(*refs):
+    sources, (out_x, out_s), held, sems = refs[:7], refs[7:9], refs[9:16], refs[16]
+    sn, sb, rn, rb, sp, an, ti = held
     depth, rows, width = sn.shape
+    order = (0, 2, 1, 3, 4, 5, 6)
+    copies = fetch([sources[n] for n in order], [held[n] for n in order], sems)
     half = rows // 2
     full = depth * rows
     odd = is_odd()
     for place, field in enumerate((sn, rn)):
+        copies[place].wait()
         value = field[...].reshape(full, width).astype(BF16)
         out_x[place * full : (place + 1) * full] = value
         out_s[place * full : (place + 1) * full] = value
@@ -62,14 +82,24 @@
         out_x[start : start + count] = jnp.where(odd, high, low)
         out_s[start : start + count] = jnp.where(odd, low, high)
 
+    copies[2].wait()
+    copies[3].wait()
     joined(sb[...], rb[...], 2 * full, full)
+    copies[4].wait()
+    copies[5].wait()
     joined(sp[...], an[...], 3 * full, full)
+    copies[6].wait()
     joined(ti[: depth // 2], ti[depth // 2 :], 4 * full, full // 2)
 
 
-def inject_kernel(grid_rows, rc, rt, sc, sw, bins, inj, bins_y, onehot, left):
+def inject_kernel(grid_rows, *refs):
+    sources, (inj, bins_y, table), held, (onehot, left, sems) = (
+        refs[:6], refs[6:9], refs[9:15], refs[15:],
+    )
+    rc, rt, sc, sw, bins, weights = held
+    copies = fetch(sources, held, sems)
     count = rc.shape[1]
-    depth, rows, width = bins.shape
+    _, rows, width = bins.shape
     first_row = lax.axis_index("gy") * rows
     half = rows // 2
     shift = width.bit_length() - 1
@@ -87,6 +117,8 @@
         edge >= grid_rows, edge - grid_rows, jnp.where(edge < 0, edge + grid_rows, edge)
     )
 
+    copies[0].wait()
+    copies[1].wait()
     for start in range(0, count, LANES):
         cells = rc[:, start : start + LANES]
         at_row = row_of(cells)
@@ -106,6 +138,8 @@
         left[...], onehot[...], (((1,), (1,)), ((), ())), preferred_element_type=F32
     )
     cols = lax.broadcasted_iota(jnp.int32, (rows, width), 1)
+    copies[2].wait()
+    copies[3].wait()
     for place, (step, wanted) in enumerate(((0, own_row), (0, edge_row), (1, own_row))):
         base = 2 * place * rows
         inj[place, 1] = spread[base : base + rows] + spread[base + rows : base + 2 * rows]
@@ -117,8 +151,16 @@
             here = jnp.logical_and(wanted == at_row, cols == at_col)
             total = total + jnp.where(here, sw[step, i], 0.0)
         inj[place, 0] = total
+    copies[4].wait()
     for y in range(rows):
         bins_y[y] = bins[:, y, :]
+    copies[5].wait()
+    lag_count, angles, bin_count, lanes = table.shape
+    values = weights[...].astype(F32)
+    for a in range(angles):
+        slab = values[:, a, :]
+        for h in range(lag_count):
+            table[h, a] = jnp.broadcast_to(slab[:, h : h + 1], (bin_count, lanes))
 
 
 def shifted_x(value, k, lane):
@@ -311,7 +353,8 @@
                     ].astype(BF16)
 
 
-def image_kernel(lags, far, near, own, chip, relay, bins, table, out, window, turned):
+def image_kernel(lags_in, far, near, own, chip, relay, bins, table, out, window, turned, lags, sems):
+    copies = fetch([lags_in], [lags], sems)
     rows, depth, width = bins.shape
     lag_count, angles = table.shape[:2]
     odd = jnp.where(is_odd(), 1, 0)
@@ -320,6 +363,7 @@
         for s in range(STEPS):
             for m in range(2):
                 window[s, m, pl.ds(block, rows)] = piece[s, m].astype(F32)
+    copies[0].wait()
     tiles = [(z, x) for z in range(0, depth, 8) for x in range(0, width, LANES)]
 
     def one_row(y, c):
@@ -371,7 +415,6 @@
 
     chip_route = [(i, i ^ 1) for i in range(size)]
     near_route = [(i, (i + 1 if i % 2 else i - 1) % size) for i in range(size)]
-    far_route = [(i, (i - 2 if i % 2 else i + 2) % size) for i in range(size)]
 
     def moved(block, route):
         return lax.ppermute(block, "gy", route)
@@ -382,26 +425,50 @@
     )
     pack_shape = jax.ShapeDtypeStruct((4 * full + full // 2, width), BF16)
     pack_x, pack_s = call(
-        pack_kernel, [pack_shape] * 2, [VMEM] * 7, [], 8, full * width * 20, full * width * 40
-    )(*fields)
+        pack_kernel,
+        [pack_shape] * 2,
+        [HBM] * 7,
+        [pltpu.VMEM((depth, rows, width), F32)] * 7 + [pltpu.SemaphoreType.DMA((7,))],
+        8,
+        full * width * 20,
+        full * width * 40,
+    )(*in_hbm(fields))
     got_s = moved(pack_s, chip_route)
     got_x = moved(pack_x, near_route)
 
-    inj, bins_y = call(
+    inj, bins_y, table = call(
         functools.partial(inject_kernel, size * rows),
         [
             jax.ShapeDtypeStruct((3, 2, rows, width), F32),
             jax.ShapeDtypeStruct((rows, depth, width), jnp.int32),
+            jax.ShapeDtypeStruct((lag_count, angles, bin_count, LANES), F32),
         ],
-        [VMEM, VMEM, SMEM, SMEM, VMEM],
-        [pltpu.VMEM((width, count), BF16), pltpu.VMEM((6 * rows, count), BF16)],
+        [HBM] * 6,
+        [
+            pltpu.VMEM((1, count), jnp.int32),
+            pltpu.VMEM((STEPS, count), F32),
+            pltpu.SMEM(source_cells.shape, jnp.int32),
+            pltpu.SMEM(source_wavelet.shape, F32),
+            pltpu.VMEM((depth, rows, width), jnp.int32),
+            pltpu.VMEM((bin_count, angles, lag_count), BF16),
+            pltpu.VMEM((width, count), BF16),
+            pltpu.VMEM((6 * rows, count), BF16),
+            pltpu.SemaphoreType.DMA((6,)),
+        ],
         8,
         12 * rows * count * width,
         full * width * 8,
-    )(receiver_cells[None], receiver_traces, source_cells, source_wavelet, angle_bins)
-    table = jnp.broadcast_to(
-        jnp.transpose(weight_table, (0, 2, 1)).astype(F32)[..., None],
-        (lag_count, angles, bin_count, LANES),
+    )(
+        *in_hbm(
+            (
+                receiver_cells[None],
+                receiver_traces,
+                source_cells,
+                source_wavelet,
+                angle_bins,
+                jnp.transpose(weight_table, (1, 2, 0)),
+            )
+        )
     )
 
     padded = (2, 2, depth + 2 * REACH, rows, width)
@@ -424,22 +491,24 @@
         full * width * 50,
     )(*fields, got_x, got_s, inj)
 
-    far = moved(own, far_route)
+    chip = moved(own, chip_route)
     near = moved(own, near_route)
-    chip = moved(own, chip_route)
+    far = moved(chip, near_route)
     relay = moved(near, chip_route)
     return call(
         image_kernel,
         jax.ShapeDtypeStruct((angles, depth, rows, width), BF16),
-        [SMEM] + [VMEM] * 7,
+        [HBM] + [VMEM] * 7,
         [
             pltpu.VMEM((STEPS, 2, 5 * rows, depth, width), F32),
             pltpu.VMEM((angles, parts, full, LANES), F32),
+            pltpu.SMEM(offset_lags.shape, jnp.int32),
+            pltpu.SemaphoreType.DMA((1,)),
         ],
         16,
         full * width * 24 * 12,
         full * width * 20,
-    )(offset_lags, far, near, own, chip, relay, bins_y, table)
+    )(*in_hbm((offset_lags,)), far, near, own, chip, relay, bins_y, table)
 
 
 def solution(mesh):

time: 40.1 us -> 37.5 us (0.935)
  the two profiles are of different devices: /device:TPU:29 before, /device:TPU:0 now
where the time goes in v1:
time: 37.5 us; the launch traced here: 37.3 us
  starting transfers between devices  15.5 us (41%)
  waiting for transfers between devices  10.9 us (29%)
  Pallas kernels  10.8 us (29%)
    ppermute x6, starting transfers between devices, moved(): return lax.ppermute(block, 'gy', route)  15.5 us
    ppermute x6, waiting for transfers between devices, moved(): return lax.ppermute(block, 'gy', route)  10.9 us
    pallas_call x1, Pallas kernels, per_device(): call(step_kernel, jax.ShapeDtypeStruct((STEPS, 2, rows, depth, width), BF...  4.12 us
    pallas_call x1, Pallas kernels, per_device(): call(image_kernel, jax.ShapeDtypeStruct((angles, depth, rows, width), BF1...  3.45 us
    pallas_call x1, Pallas kernels, per_device(): call(functools.partial(inject_kernel, size * rows), [jax.ShapeDtypeStruct...  1.81 us
    pallas_call x1, Pallas kernels, per_device(): call(pack_kernel, [pack_shape] * 2, [HBM] * 7, [pltpu.VMEM((depth, rows,...  1.39 us
  transfers between devices with their start and end apart: 6, of which 3 were waited for; matrix products, arithmetic and copies ran while one was open for 0% of the time, Pallas kernels for 5%

profile of v1, /device:TPU:0, one launch (start us, length us, event | category | flops | bytes accessed | tf_op | source)
XLA Modules:
  0.0 37.3 jit_solution(10969757908460694522)
XLA Ops:
  0.0 0.0 copy-start.1
  0.0 0.0 copy-start.2
  0.0 0.0 copy-start.3
  0.0 0.0 copy-start.4
  0.0 0.0 copy-start.5
  0.0 0.0 copy-start.6
  0.0 1.4 %shard_map.136 = (bf16[576,256]{1,0:T(8,128)(2,1)S(1)}, bf16[576,256]{1,0:T(8,128)(2,1)S(1)}) custom-call(f32[16,8,256]{2,1,0:T(8,128)} %sn.1, f32[16,8,256]{2,1,0:T(8,128)} %sb.1, f32[16,8,256]{2,1,0:T(8,128)} %rn.1, f32[16,8,256]{2,1,0:T(8,128)} %rb.1, f32[16,8,256]{2,1,0:T(8,128)} %sp.1, f32[16,8,256]{2,1,0:T(8,128)} %an.1, f32[16,8,256]{2,1,0:T(8,128)} %ti.1), custom_call_target="tpu_custom_call" | custom-call | flops 655360 | bytes 1310720 | tf_op jit(solution)/shard_map/pallas_call | solution.py:427
  1.4 0.0 copy-start
  1.4 5.6 %collective-permute-start = (bf16[576,256]{1,0:T(8,128)(2,1)S(1)}, bf16[576,256]{1,0:T(8,128)(2,1)S(1)}, u32[]{:S(2)}, u32[]{:S(2)}) collective-permute-start(bf16[576,256]{1,0:T(8,128)(2,1)S(1)} %get-tuple-element.10), channel_id=1, source_target_pairs={{0,15},{1,2},{2,1},{3,4},{4,3},{5,6},{6,5},{7,8},{8,7},{9,10},{10,... | collective-permute-start | bytes 884744 | tf_op jit(solution)/shard_map/ppermute | solution.py:420
  7.0 0.0 collective-permute-start.1
  7.0 1.8 %shard_map.137 = (f32[3,2,8,256]{3,2,1,0:T(8,128)S(1)}, s32[8,16,256]{2,1,0:T(8,128)S(1)}, f32[24,4,8,128]{3,2,1,0:T(8,128)S(1)}) custom-call(s32[1,2048]{1,0:T(1,128)} %bitcast.2, f32[2,2048]{1,0:T(2,128)} %refs_1_.3, s32[8]{0:T(128)} %refs_2_.3, f32[2,8]{1,0:T(2,128)} %refs_3_.3, s32[16,8,256]{2,1,0:T(8,128)} %refs_4_.3, bf16[8,4,24]{2,1,0:T(4,128)(2,1)} %bitcast.3), custom_call_target="tpu_custom_call" | custom-call | flops 50331648 | bytes 262144 | tf_op jit(solution)/shard_map/pallas_call | solution.py:439
  8.8 2.7 %collective-permute-done.px = bf16[576,256]{1,0:T(8,128)(2,1)S(1)} collective-permute-done((bf16[576,256]{1,0:T(8,128)(2,1)S(1)}, bf16[576,256]{1,0:T(8,128)(2,1)S(1)}, u32[]{:S(2)}, u32[]{:S(2)}) %collective-permute-start) | collective-permute-done | bytes 294944 | tf_op jit(solution)/shard_map/ppermute | solution.py:420
  11.5 0.0 collective-permute-done.1.ps
  11.5 0.0 copy-done.1
  11.5 0.0 copy-done.2
  11.5 0.0 copy-done.3
  11.5 0.0 copy-done.4
  11.5 0.0 copy-done.5
  11.5 0.0 copy-done.6
  11.5 0.0 copy-done
  11.6 4.1 %shard_map.138.own = bf16[2,2,8,16,256]{4,3,2,1,0:T(8,128)(2,1)S(1)} custom-call(f32[16,8,256]{2,1,0:T(8,128)S(1)} %copy-done, f32[16,8,256]{2,1,0:T(8,128)S(1)} %copy-done.1, f32[16,8,256]{2,1,0:T(8,128)S(1)} %copy-done.2, f32[16,8,256]{2,1,0:T(8,128)S(1)} %copy-done.3, f32[16,8,256]{2,1,0:T(8,128)S(1)} %copy-done.4, f32[16,8,256]{2,1,0:T(8,128)S(1)} %copy-done.5, ...), custom_call_target="tpu_custom_call" | custom-call | flops 19660800 | bytes 1638400 | tf_op jit(solution)/shard_map/pallas_call | solution.py:475
  15.7 4.5 %collective-permute-start.4 = (bf16[2,2,8,16,256]{4,3,2,1,0:T(8,128)(2,1)S(1)}, bf16[2,2,8,16,256]{4,3,2,1,0:T(8,128)(2,1)S(1)}, u32[]{:S(2)}, u32[]{:S(2)}) collective-permute-start(bf16[2,2,8,16,256]{4,3,2,1,0:T(8,128)(2,1)S(1)} %shard_map.138.own), channel_id=1, source_target_pairs={{0,15},{1,2},{2,1},{3,4},{4,3},{5,6},{6,5},{7,8},{8,7},{9,10},{10,... | collective-permute-start | bytes 786440 | tf_op jit(solution)/shard_map/ppermute | solution.py:420
  20.2 0.0 collective-permute-start.2
  20.2 4.2 %collective-permute-done.4.near = bf16[2,2,8,16,256]{4,3,2,1,0:T(8,128)(2,1)S(1)} collective-permute-done((bf16[2,2,8,16,256]{4,3,2,1,0:T(8,128)(2,1)S(1)}, bf16[2,2,8,16,256]{4,3,2,1,0:T(8,128)(2,1)S(1)}, u32[]{:S(2)}, u32[]{:S(2)}) %collective-permute-start.4) | collective-permute-done | bytes 262176 | tf_op jit(solution)/shard_map/ppermute | solution.py:420
  24.3 0.7 %collective-permute-start.5 = (bf16[2,2,8,16,256]{4,3,2,1,0:T(8,128)(2,1)S(1)}, bf16[2,2,8,16,256]{4,3,2,1,0:T(8,128)(2,1)S(1)}, u32[]{:S(2)}, u32[]{:S(2)}) collective-permute-start(bf16[2,2,8,16,256]{4,3,2,1,0:T(8,128)(2,1)S(1)} %collective-permute-done.4.near), channel_id=1, source_target_pairs={{0,1},{1,0},{2,3},{3,2},{4,5},{5,4},{6,7},{7,6},{8,9},{9,8},{10,11... | collective-permute-start | bytes 786440 | tf_op jit(solution)/shard_map/ppermute | solution.py:420
  25.0 0.0 collective-permute-done.2.chip
  25.0 4.8 %collective-permute-start.3 = (bf16[2,2,8,16,256]{4,3,2,1,0:T(8,128)(2,1)S(1)}, bf16[2,2,8,16,256]{4,3,2,1,0:T(8,128)(2,1)S(1)}, u32[]{:S(2)}, u32[]{:S(2)}) collective-permute-start(bf16[2,2,8,16,256]{4,3,2,1,0:T(8,128)(2,1)S(1)} %collective-permute-done.2.chip), channel_id=1, source_target_pairs={{0,15},{1,2},{2,1},{3,4},{4,3},{5,6},{6,5},{7,8},{8,7},{9,10},{10,... | collective-permute-start | bytes 786440 | tf_op jit(solution)/shard_map/ppermute | solution.py:420
  29.8 0.0 collective-permute-done.5.relay
  29.8 4.1 %collective-permute-done.3.far = bf16[2,2,8,16,256]{4,3,2,1,0:T(8,128)(2,1)S(1)} collective-permute-done((bf16[2,2,8,16,256]{4,3,2,1,0:T(8,128)(2,1)S(1)}, bf16[2,2,8,16,256]{4,3,2,1,0:T(8,128)(2,1)S(1)}, u32[]{:S(2)}, u32[]{:S(2)}) %collective-permute-start.3) | collective-permute-done | bytes 262176 | tf_op jit(solution)/shard_map/ppermute | solution.py:420
  33.9 3.5 %shard_map.139 = bf16[4,16,8,256]{3,2,1,0:T(8,128)(2,1)} custom-call(s32[24]{0:T(128)} %lags_in.1, bf16[2,2,8,16,256]{4,3,2,1,0:T(8,128)(2,1)S(1)} %collective-permute-done.3.far, bf16[2,2,8,16,256]{4,3,2,1,0:T(8,128)(2,1)S(1)} %collective-permute-done.4.near, bf16[2,2,8,16,256]{4,3,2,1,0:T(8,128)(2,1)S(1)} %shard_map.138.own, ...), custom_call_target="tpu_custom_call" | custom-call | flops 9437184 | bytes 655360 | tf_op jit(solution)/shard_map/pallas_call | solution.py:498
Async XLA Ops:
  0.0 11.5 %copy-start.1 = (f32[16,8,256]{2,1,0:T(8,128)S(1)}, f32[16,8,256]{2,1,0:T(8,128)}, u32[]{:S(2)}) copy-start(f32[16,8,256]{2,1,0:T(8,128)} %sb.1) | copy-start | bytes 393220
  0.0 11.5 %copy-start.2 = (f32[16,8,256]{2,1,0:T(8,128)S(1)}, f32[16,8,256]{2,1,0:T(8,128)}, u32[]{:S(2)}) copy-start(f32[16,8,256]{2,1,0:T(8,128)} %rn.1) | copy-start | bytes 393220
  0.0 11.5 %copy-start.3 = (f32[16,8,256]{2,1,0:T(8,128)S(1)}, f32[16,8,256]{2,1,0:T(8,128)}, u32[]{:S(2)}) copy-start(f32[16,8,256]{2,1,0:T(8,128)} %rb.1) | copy-start | bytes 393220
  0.0 11.5 %copy-start.4 = (f32[16,8,256]{2,1,0:T(8,128)S(1)}, f32[16,8,256]{2,1,0:T(8,128)}, u32[]{:S(2)}) copy-start(f32[16,8,256]{2,1,0:T(8,128)} %sp.1) | copy-start | bytes 393220
  0.0 11.5 %copy-start.5 = (f32[16,8,256]{2,1,0:T(8,128)S(1)}, f32[16,8,256]{2,1,0:T(8,128)}, u32[]{:S(2)}) copy-start(f32[16,8,256]{2,1,0:T(8,128)} %an.1) | copy-start | bytes 393220
  0.0 11.5 %copy-start.6 = (f32[16,8,256]{2,1,0:T(8,128)S(1)}, f32[16,8,256]{2,1,0:T(8,128)}, u32[]{:S(2)}) copy-start(f32[16,8,256]{2,1,0:T(8,128)} %ti.1) | copy-start | bytes 393220
  1.4 10.1 %copy-start = (f32[16,8,256]{2,1,0:T(8,128)S(1)}, f32[16,8,256]{2,1,0:T(8,128)}, u32[]{:S(2)}) copy-start(f32[16,8,256]{2,1,0:T(8,128)} %sn.1) | copy-start | bytes 393220
  1.4 10.1 %collective-permute-start = (bf16[576,256]{1,0:T(8,128)(2,1)S(1)}, bf16[576,256]{1,0:T(8,128)(2,1)S(1)}, u32[]{:S(2)}, u32[]{:S(2)}) collective-permute-start(bf16[576,256]{1,0:T(8,128)(2,1)S(1)} %get-tuple-element.10), channel_id=1, source_target_pairs={{0,15},{1,2},{2,1},{3,4},{4,3},{5,6},{6,5},{7,8},{8,7},{9,10},{10,... | collective-permute-start | bytes 884744 | tf_op jit(solution)/shard_map/ppermute | solution.py:420
  7.0 4.5 %collective-permute-start.1 = (bf16[576,256]{1,0:T(8,128)(2,1)S(1)}, bf16[576,256]{1,0:T(8,128)(2,1)S(1)}, u32[]{:S(2)}, u32[]{:S(2)}) collective-permute-start(bf16[576,256]{1,0:T(8,128)(2,1)S(1)} %get-tuple-element.11), channel_id=1, source_target_pairs={{0,1},{1,0},{2,3},{3,2},{4,5},{5,4},{6,7},{7,6},{8,9},{9,8},{10,11... | collective-permute-start | bytes 884744 | tf_op jit(solution)/shard_map/ppermute | solution.py:420
  15.7 8.7 %collective-permute-start.4 = (bf16[2,2,8,16,256]{4,3,2,1,0:T(8,128)(2,1)S(1)}, bf16[2,2,8,16,256]{4,3,2,1,0:T(8,128)(2,1)S(1)}, u32[]{:S(2)}, u32[]{:S(2)}) collective-permute-start(bf16[2,2,8,16,256]{4,3,2,1,0:T(8,128)(2,1)S(1)} %shard_map.138.own), channel_id=1, source_target_pairs={{0,15},{1,2},{2,1},{3,4},{4,3},{5,6},{6,5},{7,8},{8,7},{9,10},{10,... | collective-permute-start | bytes 786440 | tf_op jit(solution)/shard_map/ppermute | solution.py:420
  20.2 4.9 %collective-permute-start.2 = (bf16[2,2,8,16,256]{4,3,2,1,0:T(8,128)(2,1)S(1)}, bf16[2,2,8,16,256]{4,3,2,1,0:T(8,128)(2,1)S(1)}, u32[]{:S(2)}, u32[]{:S(2)}) collective-permute-start(bf16[2,2,8,16,256]{4,3,2,1,0:T(8,128)(2,1)S(1)} %shard_map.138.own), channel_id=1, source_target_pairs={{0,1},{1,0},{2,3},{3,2},{4,5},{5,4},{6,7},{7,6},{8,9},{9,8},{10,11... | collective-permute-start | bytes 786440 | tf_op jit(solution)/shard_map/ppermute | solution.py:420
  24.3 5.5 %collective-permute-start.5 = (bf16[2,2,8,16,256]{4,3,2,1,0:T(8,128)(2,1)S(1)}, bf16[2,2,8,16,256]{4,3,2,1,0:T(8,128)(2,1)S(1)}, u32[]{:S(2)}, u32[]{:S(2)}) collective-permute-start(bf16[2,2,8,16,256]{4,3,2,1,0:T(8,128)(2,1)S(1)} %collective-permute-done.4.near), channel_id=1, source_target_pairs={{0,1},{1,0},{2,3},{3,2},{4,5},{5,4},{6,7},{7,6},{8,9},{9,8},{10,11... | collective-permute-start | bytes 786440 | tf_op jit(solution)/shard_map/ppermute | solution.py:420
  25.0 8.8 %collective-permute-start.3 = (bf16[2,2,8,16,256]{4,3,2,1,0:T(8,128)(2,1)S(1)}, bf16[2,2,8,16,256]{4,3,2,1,0:T(8,128)(2,1)S(1)}, u32[]{:S(2)}, u32[]{:S(2)}) collective-permute-start(bf16[2,2,8,16,256]{4,3,2,1,0:T(8,128)(2,1)S(1)} %collective-permute-done.2.chip), channel_id=1, source_target_pairs={{0,15},{1,2},{2,1},{3,4},{4,3},{5,6},{6,5},{7,8},{8,7},{9,10},{10,... | collective-permute-start | bytes 786440 | tf_op jit(solution)/shard_map/ppermute | solution.py:420

commit v2 on v1

v2 whole, which is shorter than its diff:
```python
import functools

import jax
import jax.numpy as jnp
from jax import lax
from jax.experimental import pallas as pl
from jax.experimental.pallas import tpu as pltpu
from jax.sharding import PartitionSpec as P


STEPS = 2
SECOND = (-205.0 / 72.0, 8.0 / 5.0, -1.0 / 5.0, 8.0 / 315.0, -1.0 / 560.0)
FIRST = (4.0 / 5.0, -1.0 / 5.0, 4.0 / 105.0, -1.0 / 280.0)
REACH = 4
LANES = 128
F32 = jnp.float32
BF16 = jnp.bfloat16

VMEM = pl.BlockSpec(memory_space=pltpu.VMEM)
HBM = pl.BlockSpec(memory_space=pltpu.HBM)


def in_hbm(arrays):
    return [pltpu.with_memory_space_constraint(array, pltpu.HBM) for array in arrays]


def fetch(sources, targets, sems):
    copies = [
        pltpu.make_async_copy(source, target, sems.at[n])
        for n, (source, target) in enumerate(zip(sources, targets))
    ]
    for copy in copies:
        copy.start()
    return copies


def call(kernel, outs, in_specs, scratch, mib, flops, bytes_moved, place=VMEM):
    multiple = isinstance(outs, (list, tuple))
    return pl.pallas_call(
        kernel,
        out_shape=outs,
        in_specs=in_specs,
        out_specs=[place] * len(outs) if multiple else place,
        scratch_shapes=scratch,
        compiler_params=pltpu.CompilerParams(vmem_limit_bytes=mib << 20),
        cost_estimate=pl.CostEstimate(
            flops=flops, bytes_accessed=bytes_moved, transcendentals=0
        ),
    )


def is_odd():
    return lax.axis_index("gy") % 2 == 1


def sublane(shape):
    return lax.broadcasted_iota(jnp.int32, shape, len(shape) - 2)


def lane_parts(value):
    return [value[:, x : x + LANES] for x in range(0, value.shape[1], LANES)]


def row_roll(value, k):
    return pltpu.roll(value, k % value.shape[0], 0)


def flat_terms(value, edge, row, lane):
    parts = lane_parts(value)
    edges = None if edge is None else lane_parts(edge)
    rows = value.shape[0]
    second = [(2.0 * SECOND[0]) * part for part in parts]
    first = [None] * len(parts)
    for k in range(1, REACH + 1):
        right = [pltpu.roll(part, k, 1) for part in parts]
        left = [pltpu.roll(part, LANES - k, 1) for part in parts]
        for p, part in enumerate(parts):
            below = jnp.where(lane >= k, right[p], right[p - 1] if p else 0.0)
            above = jnp.where(lane < LANES - k, left[p], left[p + 1] if p + 1 < len(parts) else 0.0)
            outer_up = 0.0 if edges is None else row_roll(edges[p], -k)
            outer_down = 0.0 if edges is None else row_roll(edges[p], k)
            up = jnp.where(row < rows - k, row_roll(part, -k), outer_up)
            down = jnp.where(row >= k, row_roll(part, k), outer_down)
            second[p] = second[p] + SECOND[k] * ((above + below) + (up + down))
            term = FIRST[k - 1] * ((above - below) + (up - down))
            first[p] = term if first[p] is None else first[p] + term
    return second, first


def cross_terms(edge, row, sign):
    rows = edge.shape[0]
    second, first = [], []
    for part in lane_parts(edge):
        a = b = None
        for k in range(1, REACH + 1):
            value = jnp.where(
                row < k, row_roll(part, k), jnp.where(row >= rows - k, row_roll(part, -k), 0.0)
            )
            a = SECOND[k] * value if a is None else a + SECOND[k] * value
            b = FIRST[k - 1] * value if b is None else b + FIRST[k - 1] * value
        second.append(a)
        first.append(sign * b)
    return second, first


def depth_second(field, at):
    second = SECOND[0] * field[at + REACH]
    for k in range(1, REACH + 1):
        second = second + SECOND[k] * (field[at + REACH + k] + field[at + REACH - k])
    return second


def depth_first(slope, at):
    first = None
    for k in range(1, REACH + 1):
        term = FIRST[k - 1] * (slope[at + REACH + k] - slope[at + REACH - k])
        first = term if first is None else first + term
    return first


def clear_ends(ref):
    depth = ref.shape[0] - 2 * REACH
    zeros = jnp.zeros((REACH,) + ref.shape[1:], F32)
    ref[:REACH] = zeros
    ref[REACH + depth :] = zeros


def pack_kernel(*refs):
    sources, (out_x, out_s, partial, flat_factor, tilt_factor), rest = refs[:7], refs[7:12], refs[12:]
    (sn, rn, sb, rb, sp, an, ti, slope, base), sems = rest[:9], rest[9]
    depth, rows, width = sp.shape
    half = rows // 2
    full = depth * rows
    odd = is_odd()
    row = sublane((rows, LANES))
    lane = lax.broadcasted_iota(jnp.int32, (rows, LANES), 1)
    order = (0, 2, 1, 3, 4, 5, 6)
    chunk = depth // 2
    inner = pl.ds(REACH, depth)
    targets = (sn.at[inner], rn.at[inner], sb, rb, sp, an, ti)
    copies = []
    for c in range(2):
        span = pl.ds(c * chunk, chunk)
        copies.append(
            fetch(
                [sources[n].at[span] for n in order],
                [target.at[span] for target in targets],
                sems.at[c],
            )
        )
    for ref in (sn, rn):
        clear_ends(ref)
    for m in range(2):
        clear_ends(slope.at[m])

    def flat(z, c):
        factor = sp[z] * (1.0 + 2.0 * an[z])
        flat_factor[z] = factor
        tilt_factor[z] = sp[z] * ti[z]
        for m, (now, before) in enumerate(((sn, sb), (rn, rb))):
            value = now[z + REACH]
            second, first = flat_terms(value, None, row, lane)
            for p in range(width // LANES):
                lanes = slice(p * LANES, (p + 1) * LANES)
                slope[m, z + REACH, :, lanes] = first[p]
                base[m, z, :, lanes] = (
                    2.0 * value[:, lanes] - before[z, :, lanes] + factor[:, lanes] * second[p]
                )
        return c

    for c in range(2):
        for copy in copies[c]:
            copy.wait()
        lax.fori_loop(c * chunk, (c + 1) * chunk, flat, 0, unroll=2)

    def deep(z, c):
        for m, now in enumerate((sn, rn)):
            partial[m, z] = (
                base[m, z]
                + sp[z] * depth_second(now, z)
                + tilt_factor[z] * depth_first(slope.at[m], z)
            )
        return c

    lax.fori_loop(0, depth, deep, 0, unroll=2)
    first_half = sublane((depth, rows, width)) < half

    def joined(a, b, place):
        turned_a = pltpu.roll(a, half, 1)
        turned_b = pltpu.roll(b, half, 1)
        low = jnp.where(first_half, a, turned_b).reshape(full, width).astype(BF16)
        high = jnp.where(first_half, turned_a, b).reshape(full, width).astype(BF16)
        out_x[place * full : (place + 1) * full] = jnp.where(odd, high, low)
        out_s[place * full : (place + 1) * full] = jnp.where(odd, low, high)

    joined(sn[REACH : REACH + depth], rn[REACH : REACH + depth], 0)
    joined(partial[0], partial[1], 1)
    joined(flat_factor[...], tilt_factor[...], 2)


def inject_kernel(grid_rows, *refs):
    sources, now, (inj, bins_y, table, edge_flat, edge_slope), held, (onehot, left, sems) = (
        refs[:6], refs[6:8], refs[8:13], refs[13:19], refs[19:],
    )
    rc, rt, sc, sw, bins, weights = held
    copies = fetch(sources, held, sems)
    count = rc.shape[1]
    depth, rows, width = bins.shape
    first_row = lax.axis_index("gy") * rows
    half = rows // 2
    shift = width.bit_length() - 1
    power = 1 << shift == width

    def row_of(cell):
        if power:
            return lax.shift_right_logical(cell, jnp.int32(shift))
        return lax.div(cell, jnp.int32(width))

    own = lax.broadcasted_iota(jnp.int32, (rows, 1), 0)
    own_row = first_row + own
    edge = first_row + jnp.where(own < half, own + rows, own - rows)
    edge_row = jnp.where(
        edge >= grid_rows, edge - grid_rows, jnp.where(edge < 0, edge + grid_rows, edge)
    )

    copies[0].wait()
    copies[1].wait()
    for start in range(0, count, LANES):
        cells = rc[:, start : start + LANES]
        at_row = row_of(cells)
        at_col = cells - at_row * width
        cols = lax.broadcasted_iota(jnp.int32, (width, LANES), 0)
        onehot[:, start : start + LANES] = jnp.where(cols == at_col, 1.0, 0.0).astype(BF16)
        parts = []
        for step, wanted in ((0, own_row), (0, edge_row), (1, own_row)):
            amount = rt[step : step + 1, start : start + LANES]
            coarse = amount.astype(BF16).astype(F32)
            fine = amount - coarse
            here = wanted == at_row
            parts.append(jnp.where(here, coarse, 0.0))
            parts.append(jnp.where(here, fine, 0.0))
        left[:, start : start + LANES] = jnp.concatenate(parts, 0).astype(BF16)
    spread = lax.dot_general(
        left[...], onehot[...], (((1,), (1,)), ((), ())), preferred_element_type=F32
    )
    cols = lax.broadcasted_iota(jnp.int32, (rows, width), 1)
    copies[2].wait()
    copies[3].wait()
    for place, (step, wanted) in enumerate(((0, own_row), (0, edge_row), (1, own_row))):
        base = 2 * place * rows
        inj[place, 1] = spread[base : base + rows] + spread[base + rows : base + 2 * rows]
        total = jnp.zeros((rows, width), F32)
        for i in range(sc.shape[0]):
            cell = sc[i]
            at_row = lax.div(cell, jnp.int32(width))
            at_col = cell - at_row * width
            here = jnp.logical_and(wanted == at_row, cols == at_col)
            total = total + jnp.where(here, sw[step, i], 0.0)
        inj[place, 0] = total
    copies[4].wait()
    for y in range(rows):
        bins_y[y] = bins[:, y, :]
    copies[5].wait()
    table_rows, angles, bin_count, lanes = table.shape
    lag_count = table_rows - 1
    table[lag_count] = jnp.zeros((angles, bin_count, lanes), F32)
    values = weights[...].astype(F32)
    for a in range(angles):
        slab = values[:, a, :]
        for h in range(lag_count):
            table[h, a] = jnp.broadcast_to(slab[:, h : h + 1], (bin_count, lanes))
    row = sublane((rows, LANES))
    sign = jnp.where(row < half, -1.0, 1.0)
    for m in range(2):
        clear_ends(edge_slope.at[m])

        def edge(z, c, m=m):
            second, first = cross_terms(now[m][z], row, sign)
            for p in range(width // LANES):
                lanes = slice(p * LANES, (p + 1) * LANES)
                edge_flat[m, z, :, lanes] = second[p]
                edge_slope[m, z + REACH, :, lanes] = first[p]
            return c

        lax.fori_loop(0, depth, edge, 0, unroll=2)


def step_kernel(
    sn, rn, sp, partial, flat_factor, tilt_factor, edge_flat, edge_slope, px, ps, inj, out,
    slope, base, edge_base, edge_tilt, later, later_edge, turned,
):
    depth, rows, width = sn.shape
    half = rows // 2
    full = depth * rows
    odd = is_odd()
    row = sublane((rows, LANES))
    lane = lax.broadcasted_iota(jnp.int32, (rows, LANES), 1)
    sign = jnp.where(row < half, -1.0, 1.0)
    low_half = sublane((rows, width)) < half
    now = (sn, rn)
    parts = [slice(x, x + LANES) for x in range(0, width, LANES)]
    for m in range(2):
        clear_ends(slope.at[m])
        clear_ends(later.at[m])

    def from_packs(start):
        x = px[pl.ds(start, 2 * rows), :].astype(F32)
        s = ps[pl.ds(start, 2 * rows), :].astype(F32)
        return jnp.where(odd, s, x), jnp.where(odd, x, s)

    def edge_pair(low, high):
        first = jnp.where(low_half, high, row_roll(low, half))
        second = jnp.where(low_half, row_roll(high, half), low)
        return first, second

    def flat(pair, c):
        got = [
            from_packs(pl.multiple_of(n * full + pair * 2 * rows, 2 * rows)) for n in range(3)
        ]
        for j in range(2):
            part = slice(j * rows, (j + 1) * rows)
            z = 2 * pair + j
            edges, partials, factors = [edge_pair(low[part], high[part]) for low, high in got]
            edge_tilt[z] = factors[1]
            for m in range(2):
                edge_base[m, z] = partials[m] + factors[0] * edge_flat[m, z]
                second, first = cross_terms(edges[m], row, sign)
                for p, lanes in enumerate(parts):
                    slope[m, z + REACH, :, lanes] = first[p]
                    base[m, z, :, lanes] = (
                        partial[m, z, :, lanes] + flat_factor[z, :, lanes] * second[p]
                    )
        return c

    lax.fori_loop(0, depth // 2, flat, 0)

    def deep(z, c):
        for m in range(2):
            later[m, z + REACH] = base[m, z] + tilt_factor[z] * depth_first(slope.at[m], z)
            later_edge[m, z] = edge_base[m, z] + edge_tilt[z] * depth_first(edge_slope.at[m], z)
        return c

    lax.fori_loop(0, depth, deep, 0, unroll=2)
    for m in range(2):
        later[m, REACH] = later[m, REACH] + inj[0, m]
        later_edge[m, 0] = later_edge[m, 0] + inj[1, m]

    def flat_later(z, c):
        for m in range(2):
            mid = later[m, z + REACH]
            second, first = flat_terms(mid, later_edge[m, z], row, lane)
            for p, lanes in enumerate(parts):
                slope[m, z + REACH, :, lanes] = first[p]
                base[m, z, :, lanes] = (
                    2.0 * mid[:, lanes]
                    - now[m][z, :, lanes]
                    + flat_factor[z, :, lanes] * second[p]
                )
                turned[0, m, p, pl.ds(z, rows, stride=depth), :] = mid[:, lanes]
        return c

    lax.fori_loop(0, depth, flat_later, 0, unroll=2)

    def deep_later(z, c):
        surface = jnp.where(z == 0, 1.0, 0.0)
        for m in range(2):
            value = (
                base[m, z]
                + sp[z] * depth_second(later.at[m], z)
                + tilt_factor[z] * depth_first(slope.at[m], z)
                + surface * inj[2, m]
            )
            for p, lanes in enumerate(parts):
                turned[1, m, p, pl.ds(z, rows, stride=depth), :] = value[:, lanes]
        return c

    lax.fori_loop(0, depth, deep_later, 0, unroll=2)
    for s in range(STEPS):
        for m in range(2):
            for p, lanes in enumerate(parts):
                for y in range(rows):
                    out[s, m, y, :, lanes] = turned[
                        s, m, p, y * depth : (y + 1) * depth, :
                    ].astype(BF16)


GROUP = 4


def listed(lags, rows, near, picks):
    count = jnp.int32(0)
    total = lags.shape[0]
    for h in range(total):
        lag = lags[h]
        inside = jnp.logical_and(lag <= rows, lag >= -rows)
        picks[0, count] = lag
        picks[1, count] = h
        count = count + jnp.where(inside == near, 1, 0)
    for n in range(GROUP):
        picks[0, count + n] = 0
        picks[1, count + n] = total
    return count


def add_lags(window, table, ids, picks, groups, y, rows, tiles, sums):
    steps = window.shape[0]
    angles = table.shape[1]
    at = y + rows * 2

    def one_group(group, sums):
        sums = [list(a) for a in sums]
        for member in range(GROUP):
            lag = picks[0, group * GROUP + member]
            h = picks[1, group * GROUP + member]
            for n, (z, x) in enumerate(tiles):
                zs, xs = slice(z, z + 8), slice(x, x + LANES)
                product = None
                for s in range(steps):
                    term = window[s, 0, at - lag, zs, xs] * window[s, 1, at + lag, zs, xs]
                    product = term if product is None else product + term
                for a in range(angles):
                    weight = jnp.take_along_axis(
                        table[h, a], ids[n], axis=0, mode="promise_in_bounds"
                    )
                    sums[a][n] = sums[a][n] + weight * product
        return tuple(tuple(a) for a in sums)

    return lax.fori_loop(0, groups, one_group, sums)


def place_pieces(window, pieces, rows):
    odd = jnp.where(is_odd(), 1, 0)
    for piece, place in pieces:
        block = (place + odd * (4 - 2 * place)) * rows
        for s in range(STEPS):
            for m in range(2):
                window[s, m, pl.ds(block, rows)] = piece[s, m].astype(F32)


def near_image_kernel(
    lags_in, near, own, chip, bins, table, out, far_picks, window, lags, picks, sems
):
    copies = fetch([lags_in], [lags], sems)
    rows, depth, width = bins.shape
    angles = table.shape[1]
    place_pieces(window, ((near, 1), (own, 2), (chip, 3)), rows)
    copies[0].wait()
    count = listed(lags, rows, False, picks)
    row = lax.broadcasted_iota(jnp.int32, far_picks.shape, 0)
    lane = lax.broadcasted_iota(jnp.int32, far_picks.shape, 1)
    held = jnp.where(row == 2, count, 0)
    for n in range(lags.shape[0] + GROUP):
        value = jnp.where(row == 0, picks[0, n], picks[1, n])
        held = jnp.where(jnp.logical_and(lane == n, row < 2), value, held)
    far_picks[...] = held
    count = listed(lags, rows, True, picks)
    groups = lax.div(count + (GROUP - 1), GROUP)
    tiles = [(z, x) for z in range(0, depth, 8) for x in range(0, width, LANES)]
    zero = jnp.zeros((8, LANES), F32)

    def one_row(y, c):
        ids = [bins[y, z : z + 8, x : x + LANES] for z, x in tiles]
        sums = tuple((zero,) * len(tiles) for _ in range(angles))
        sums = add_lags(window, table, ids, picks, groups, y, rows, tiles, sums)
        for a in range(angles):
            for n, (z, x) in enumerate(tiles):
                out[a, y, z : z + 8, x : x + LANES] = sums[a][n]
        return c

    lax.fori_loop(0, rows, one_row, 0)


def far_image_kernel(
    before, picks_in, far, near, own, chip, relay, bins, table, out,
    window, turned, staged, picks, sems,
):
    pick = pltpu.make_async_copy(picks_in, picks, sems.at[0])
    pick.start()
    rows, depth, width = bins.shape
    angles = table.shape[1]
    place_pieces(window, ((far, 0), (near, 1), (own, 2), (chip, 3), (relay, 4)), rows)
    pick.wait()
    groups = lax.div(picks[2, 0] + (GROUP - 1), GROUP)
    sends = []
    for part in range(width // LANES):
        lanes = slice(part * LANES, (part + 1) * LANES)
        tiles = [(z, part * LANES) for z in range(0, depth, 8)]

        def one_row(y, c, tiles=tiles, lanes=lanes):
            ids = [bins[y, z : z + 8, lanes] for z, _ in tiles]
            sums = tuple(
                tuple(before[a, y, z : z + 8, lanes] for z, _ in tiles) for a in range(angles)
            )
            sums = add_lags(window, table, ids, picks, groups, y, rows, tiles, sums)
            for a in range(angles):
                for n, (z, _) in enumerate(tiles):
                    turned[a, pl.ds(z * rows + y, 8, stride=rows), :] = sums[a][n]
            return c

        lax.fori_loop(0, rows, one_row, 0)
        for a in range(angles):
            staged[part, a] = turned[a].astype(BF16).reshape(depth, rows, LANES)
        send = pltpu.make_async_copy(
            staged.at[part], out.at[:, :, :, lanes], sems.at[1 + part]
        )
        send.start()
        sends.append(send)
    for send in sends:
        send.wait()


def per_device(
    source_now, source_before, receiver_now, receiver_before, speed_term, aniso_field,
    tilt_field, angle_bins, weight_table, offset_lags, source_cells, source_wavelet,
    receiver_cells, receiver_traces,
):
    depth, rows, width = source_now.shape
    size = lax.axis_size("gy")
    full = depth * rows
    lag_count, bin_count, angles = weight_table.shape
    count = receiver_cells.shape[0]
    parts = width // LANES

    chip_route = [(i, i ^ 1) for i in range(size)]
    near_route = [(i, (i + 1 if i % 2 else i - 1) % size) for i in range(size)]

    def moved(block, route):
        return lax.ppermute(block, "gy", route)

    fields = (
        source_now, source_before, receiver_now, receiver_before, speed_term, aniso_field,
        tilt_field,
    )
    tall = depth + 2 * REACH
    grid = (depth, rows, width)
    pack_shape = jax.ShapeDtypeStruct((3 * full, width), BF16)
    pack_x, pack_s, partial, flat_factor, tilt_factor = call(
        pack_kernel,
        [
            pack_shape,
            pack_shape,
            jax.ShapeDtypeStruct((2,) + grid, F32),
            jax.ShapeDtypeStruct(grid, F32),
            jax.ShapeDtypeStruct(grid, F32),
        ],
        [HBM] * 7,
        [pltpu.VMEM((tall, rows, width), F32)] * 2
        + [pltpu.VMEM(grid, F32)] * 5
        + [
            pltpu.VMEM((2, tall, rows, width), F32),
            pltpu.VMEM((2,) + grid, F32),
            pltpu.SemaphoreType.DMA((2, 7)),
        ],
        8,
        full * width * 200,
        full * width * 40,
    )(*in_hbm(fields))
    got_s = moved(pack_s, chip_route)
    got_x = moved(pack_x, near_route)

    inj, bins_y, table, edge_flat, edge_slope = call(
        functools.partial(inject_kernel, size * rows),
        [
            jax.ShapeDtypeStruct((3, 2, rows, width), F32),
            jax.ShapeDtypeStruct((rows, depth, width), jnp.int32),
            jax.ShapeDtypeStruct((lag_count + 1, angles, bin_count, LANES), F32),
            jax.ShapeDtypeStruct((2,) + grid, F32),
            jax.ShapeDtypeStruct((2, tall, rows, width), F32),
        ],
        [HBM] * 6 + [VMEM] * 2,
        [
            pltpu.VMEM((1, count), jnp.int32),
            pltpu.VMEM((STEPS, count), F32),
            pltpu.SMEM(source_cells.shape, jnp.int32),
            pltpu.SMEM(source_wavelet.shape, F32),
            pltpu.VMEM((depth, rows, width), jnp.int32),
            pltpu.VMEM((bin_count, angles, lag_count), BF16),
            pltpu.VMEM((width, count), BF16),
            pltpu.VMEM((6 * rows, count), BF16),
            pltpu.SemaphoreType.DMA((6,)),
        ],
        8,
        12 * rows * count * width,
        full * width * 8,
    )(
        *in_hbm(
            (
                receiver_cells[None],
                receiver_traces,
                source_cells,
                source_wavelet,
                angle_bins,
                jnp.transpose(weight_table, (1, 2, 0)),
            )
        ),
        source_now,
        receiver_now,
    )

    own = call(
        step_kernel,
        jax.ShapeDtypeStruct((STEPS, 2, rows, depth, width), BF16),
        [VMEM] * 11,
        [
            pltpu.VMEM((2, tall, rows, width), F32),
            pltpu.VMEM((2,) + grid, F32),
            pltpu.VMEM((2,) + grid, F32),
            pltpu.VMEM(grid, F32),
            pltpu.VMEM((2, tall, rows, width), F32),
            pltpu.VMEM((2,) + grid, F32),
            pltpu.VMEM((STEPS, 2, parts, full, LANES), F32),
        ],
        16,
        full * width * 300,
        full * width * 50,
    )(
        source_now, receiver_now, speed_term, partial, flat_factor, tilt_factor, edge_flat,
        edge_slope, got_x, got_s, inj,
    )

    chip = moved(own, chip_route)
    near = moved(own, near_route)
    far = moved(chip, near_route)
    relay = moved(near, chip_route)
    window = pltpu.VMEM((STEPS, 2, 5 * rows, depth, width), F32)
    pick_space = pltpu.SMEM((8, LANES), jnp.int32)
    half_image, far_picks = call(
        near_image_kernel,
        [
            jax.ShapeDtypeStruct((angles, rows, depth, width), F32),
            jax.ShapeDtypeStruct((8, LANES), jnp.int32),
        ],
        [HBM] + [VMEM] * 5,
        [
            window,
            pltpu.SMEM(offset_lags.shape, jnp.int32),
            pick_space,
            pltpu.SemaphoreType.DMA((1,)),
        ],
        16,
        full * width * lag_count * 6,
        full * width * 20,
    )(*in_hbm((offset_lags,)), near, own, chip, bins_y, table)
    return call(
        far_image_kernel,
        jax.ShapeDtypeStruct((angles, depth, rows, width), BF16),
        [VMEM] * 9,
        [
            window,
            pltpu.VMEM((angles, full, LANES), F32),
            pltpu.VMEM((parts, angles, depth, rows, LANES), BF16),
            pick_space,
            pltpu.SemaphoreType.DMA((1 + parts,)),
        ],
        16,
        full * width * lag_count * 6,
        full * width * 20,
        HBM,
    )(half_image, far_picks, far, near, own, chip, relay, bins_y, table)


def solution(mesh):
    grid = P("shot", "gy", None)
    media = P(None, "gy", None)
    return jax.shard_map(
        per_device,
        mesh=mesh,
        in_specs=(grid,) * 4
        + (media,) * 4
        + (P(), P(), P("shot"), P("shot", None), P("shot"), P("shot", None)),
        out_specs=P("shot", None, "gy", None),
        check_vma=False,
    )
```

time: 37.5 us -> 31.6 us (0.84)
  the two profiles are of different devices: /device:TPU:0 before, /device:TPU:1 now
where the time goes in v2:
time: 31.6 us; the launch traced here: 31.4 us
  Pallas kernels  12.5 us (40%)
  waiting for transfers between devices  9.71 us (31%)
  starting transfers between devices  9.15 us (29%)
    ppermute x6, waiting for transfers between devices, moved(): return lax.ppermute(block, 'gy', route)  9.71 us
    ppermute x6, starting transfers between devices, moved(): return lax.ppermute(block, 'gy', route)  9.15 us
    pallas_call x1, Pallas kernels, per_device(): call(far_image_kernel, jax.ShapeDtypeStruct((angles, depth, rows, width),...  3.16 us
    pallas_call x1, Pallas kernels, per_device(): call(pack_kernel, [pack_shape, pack_shape, jax.ShapeDtypeStruct((2,) + gr...  2.72 us
    pallas_call x1, Pallas kernels, per_device(): call(step_kernel, jax.ShapeDtypeStruct((STEPS, 2, rows, depth, width), BF...  2.3 us
    pallas_call x1, Pallas kernels, per_device(): call(functools.partial(inject_kernel, size * rows), [jax.ShapeDtypeStruct...  2.18 us
    pallas_call x1, Pallas kernels, per_device(): call(near_image_kernel, [jax.ShapeDtypeStruct((angles, rows, depth, width...  2.1 us
  transfers between devices with their start and end apart: 6, of which 3 were waited for; matrix products, arithmetic and copies ran while one was open for 0% of the time, Pallas kernels for 14%

profile of v2, /device:TPU:1, one launch (start us, length us, event | category | flops | bytes accessed | tf_op | source)
XLA Modules:
  0.0 31.4 jit_solution(5894403544414308893)
XLA Ops:
  0.0 0.0 copy-start.1
  0.0 0.0 copy-start
  0.0 2.7 %shard_map.136 = (bf16[384,256]{1,0:T(8,128)(2,1)S(1)}, bf16[384,256]{1,0:T(8,128)(2,1)S(1)}, f32[2,16,8,256]{3,2,1,0:T(8,128)S(1)}, f32[16,8,256]{2,1,0:T(8,128)S(1)}, f32[16,8,256]{2,1,0:T(8,128)S(1)}) custom-call(f32[16,8,256]{2,1,0:T(8,128)} %sn.1, f32[16,8,256]{2,1,0:T(8,128)} %refs_1_.2, f32[16,8,256]{2,1,0:T(8,128)} %rn.1, f32[16,8,256]{2,1,0:T(8,128)} %refs_3_.2, ...), custom_call_target="tpu_custom_call" | custom-call | flops 6553600 | bytes 1310720 | tf_op jit(solution)/shard_map/pallas_call | solution.py:537
  2.7 2.7 %collective-permute-start = (bf16[384,256]{1,0:T(8,128)(2,1)S(1)}, bf16[384,256]{1,0:T(8,128)(2,1)S(1)}, u32[]{:S(2)}, u32[]{:S(2)}) collective-permute-start(bf16[384,256]{1,0:T(8,128)(2,1)S(1)} %get-tuple-element.22), channel_id=1, source_target_pairs={{0,15},{1,2},{2,1},{3,4},{4,3},{5,6},{6,5},{7,8},{8,7},{9,10},{10,... | collective-permute-start | bytes 589832 | tf_op jit(solution)/shard_map/ppermute | solution.py:528
  5.4 2.9 %collective-permute-start.1 = (bf16[384,256]{1,0:T(8,128)(2,1)S(1)}, bf16[384,256]{1,0:T(8,128)(2,1)S(1)}, u32[]{:S(2)}, u32[]{:S(2)}) collective-permute-start(bf16[384,256]{1,0:T(8,128)(2,1)S(1)} %get-tuple-element.23), channel_id=1, source_target_pairs={{0,1},{1,0},{2,3},{3,2},{4,5},{5,4},{6,7},{7,6},{8,9},{9,8},{10,11... | collective-permute-start | bytes 589832 | tf_op jit(solution)/shard_map/ppermute | solution.py:528
  8.3 0.0 copy-done.1
  8.3 0.0 copy-done
  8.3 0.0 copy-start.2
  8.3 2.2 %shard_map.137 = (f32[3,2,8,256]{3,2,1,0:T(8,128)S(1)}, s32[8,16,256]{2,1,0:T(8,128)S(1)}, f32[25,4,8,128]{3,2,1,0:T(8,128)S(1)}, f32[2,16,8,256]{3,2,1,0:T(8,128)S(1)}, f32[2,24,8,256]{3,2,1,0:T(8,128)S(1)}) custom-call(s32[1,2048]{1,0:T(1,128)} %bitcast.2, f32[2,2048]{1,0:T(2,128)} %refs_1_.3, s32[8]{0:T(128)} %refs_2_.3, f32[2,8]{1,0:T(2,128)} %refs_3_.3, ...), custom_call_target="tpu_custom_call" | custom-call | flops 50331648 | bytes 262144 | tf_op jit(solution)/shard_map/pallas_call | solution.py:561
  10.5 0.0 collective-permute-done.px
  10.5 0.0 collective-permute-done.1.ps
  10.5 0.0 copy-done.2
  10.5 2.3 %shard_map.138.own = bf16[2,2,8,16,256]{4,3,2,1,0:T(8,128)(2,1)S(1)} custom-call(f32[16,8,256]{2,1,0:T(8,128)S(1)} %copy-done, f32[16,8,256]{2,1,0:T(8,128)S(1)} %copy-done.1, f32[16,8,256]{2,1,0:T(8,128)S(1)} %copy-done.2, f32[2,16,8,256]{3,2,1,0:T(8,128)S(1)} %get-tuple-element.17.partial, f32[16,8,256]{2,1,0:T(8,128)S(1)} %get-tuple-element.18.flat_factor, ...), custom_call_target="tpu_custom_call" | custom-call | flops 9830400 | bytes 1638400 | tf_op jit(solution)/shard_map/pallas_call | solution.py:600
  12.8 1.2 %collective-permute-start.3 = (bf16[2,2,8,16,256]{4,3,2,1,0:T(8,128)(2,1)S(1)}, bf16[2,2,8,16,256]{4,3,2,1,0:T(8,128)(2,1)S(1)}, u32[]{:S(2)}, u32[]{:S(2)}) collective-permute-start(bf16[2,2,8,16,256]{4,3,2,1,0:T(8,128)(2,1)S(1)} %shard_map.138.own), channel_id=1, source_target_pairs={{0,1},{1,0},{2,3},{3,2},{4,5},{5,4},{6,7},{7,6},{8,9},{9,8},{10,11... | collective-permute-start | bytes 786440 | tf_op jit(solution)/shard_map/ppermute | solution.py:528
  14.0 1.1 %collective-permute-start.2 = (bf16[2,2,8,16,256]{4,3,2,1,0:T(8,128)(2,1)S(1)}, bf16[2,2,8,16,256]{4,3,2,1,0:T(8,128)(2,1)S(1)}, u32[]{:S(2)}, u32[]{:S(2)}) collective-permute-start(bf16[2,2,8,16,256]{4,3,2,1,0:T(8,128)(2,1)S(1)} %shard_map.138.own), channel_id=1, source_target_pairs={{0,15},{1,2},{2,1},{3,4},{4,3},{5,6},{6,5},{7,8},{8,7},{9,10},{10,... | collective-permute-start | bytes 786440 | tf_op jit(solution)/shard_map/ppermute | solution.py:528
  15.1 0.1 collective-permute-done.3.chip
  15.2 1.3 %collective-permute-start.4 = (bf16[2,2,8,16,256]{4,3,2,1,0:T(8,128)(2,1)S(1)}, bf16[2,2,8,16,256]{4,3,2,1,0:T(8,128)(2,1)S(1)}, u32[]{:S(2)}, u32[]{:S(2)}) collective-permute-start(bf16[2,2,8,16,256]{4,3,2,1,0:T(8,128)(2,1)S(1)} %collective-permute-done.3.chip), channel_id=1, source_target_pairs={{0,15},{1,2},{2,1},{3,4},{4,3},{5,6},{6,5},{7,8},{8,7},{9,10},{10,... | collective-permute-start | bytes 786440 | tf_op jit(solution)/shard_map/ppermute | solution.py:528
  16.5 7.5 %collective-permute-done.2.near = bf16[2,2,8,16,256]{4,3,2,1,0:T(8,128)(2,1)S(1)} collective-permute-done((bf16[2,2,8,16,256]{4,3,2,1,0:T(8,128)(2,1)S(1)}, bf16[2,2,8,16,256]{4,3,2,1,0:T(8,128)(2,1)S(1)}, u32[]{:S(2)}, u32[]{:S(2)}) %collective-permute-start.2) | collective-permute-done | bytes 262176 | tf_op jit(solution)/shard_map/ppermute | solution.py:528
  24.0 0.0 collective-permute-start.5
  24.0 2.1 %shard_map.139 = (f32[4,8,16,256]{3,2,1,0:T(8,128)S(1)}, s32[8,128]{1,0:T(8,128)S(1)}) custom-call(s32[24]{0:T(128)} %lags_in.1, bf16[2,2,8,16,256]{4,3,2,1,0:T(8,128)(2,1)S(1)} %collective-permute-done.2.near, bf16[2,2,8,16,256]{4,3,2,1,0:T(8,128)(2,1)S(1)} %shard_map.138.own, bf16[2,2,8,16,256]{4,3,2,1,0:T(8,128)(2,1)S(1)} %collective-permute-done.3.chip, ...), custom_call_target="tpu_custom_call" | custom-call | flops 4718592 | bytes 655360 | tf_op jit(solution)/shard_map/pallas_call | solution.py:627
  26.1 2.1 %collective-permute-done.4.far = bf16[2,2,8,16,256]{4,3,2,1,0:T(8,128)(2,1)S(1)} collective-permute-done((bf16[2,2,8,16,256]{4,3,2,1,0:T(8,128)(2,1)S(1)}, bf16[2,2,8,16,256]{4,3,2,1,0:T(8,128)(2,1)S(1)}, u32[]{:S(2)}, u32[]{:S(2)}) %collective-permute-start.4) | collective-permute-done | bytes 262176 | tf_op jit(solution)/shard_map/ppermute | solution.py:528
  28.2 0.0 collective-permute-done.5.relay
  28.2 3.2 %shard_map.140 = bf16[4,16,8,256]{3,2,1,0:T(8,128)(2,1)} custom-call(f32[4,8,16,256]{3,2,1,0:T(8,128)S(1)} %get-tuple-element.27.before, s32[8,128]{1,0:T(8,128)S(1)} %get-tuple-element.28.picks_in, bf16[2,2,8,16,256]{4,3,2,1,0:T(8,128)(2,1)S(1)} %collective-permute-done.4.far, bf16[2,2,8,16,256]{4,3,2,1,0:T(8,128)(2,1)S(1)} %collective-permute-done.2.near, ...), custom_call_target="tpu_custom_call" | custom-call | flops 4718592 | bytes 655360 | tf_op jit(solution)/shard_map/pallas_call | solution.py:644
Async XLA Ops:
  0.0 8.3 %copy-start.1 = (f32[16,8,256]{2,1,0:T(8,128)S(1)}, f32[16,8,256]{2,1,0:T(8,128)}, u32[]{:S(2)}) copy-start(f32[16,8,256]{2,1,0:T(8,128)} %rn.1) | copy-start | bytes 393220
  0.0 8.3 %copy-start = (f32[16,8,256]{2,1,0:T(8,128)S(1)}, f32[16,8,256]{2,1,0:T(8,128)}, u32[]{:S(2)}) copy-start(f32[16,8,256]{2,1,0:T(8,128)} %sn.1) | copy-start | bytes 393220
  2.7 7.8 %collective-permute-start = (bf16[384,256]{1,0:T(8,128)(2,1)S(1)}, bf16[384,256]{1,0:T(8,128)(2,1)S(1)}, u32[]{:S(2)}, u32[]{:S(2)}) collective-permute-start(bf16[384,256]{1,0:T(8,128)(2,1)S(1)} %get-tuple-element.22), channel_id=1, source_target_pairs={{0,15},{1,2},{2,1},{3,4},{4,3},{5,6},{6,5},{7,8},{8,7},{9,10},{10,... | collective-permute-start | bytes 589832 | tf_op jit(solution)/shard_map/ppermute | solution.py:528
  5.4 5.1 %collective-permute-start.1 = (bf16[384,256]{1,0:T(8,128)(2,1)S(1)}, bf16[384,256]{1,0:T(8,128)(2,1)S(1)}, u32[]{:S(2)}, u32[]{:S(2)}) collective-permute-start(bf16[384,256]{1,0:T(8,128)(2,1)S(1)} %get-tuple-element.23), channel_id=1, source_target_pairs={{0,1},{1,0},{2,3},{3,2},{4,5},{5,4},{6,7},{7,6},{8,9},{9,8},{10,11... | collective-permute-start | bytes 589832 | tf_op jit(solution)/shard_map/ppermute | solution.py:528
  8.3 2.2 %copy-start.2 = (f32[16,8,256]{2,1,0:T(8,128)S(1)}, f32[16,8,256]{2,1,0:T(8,128)}, u32[]{:S(2)}) copy-start(f32[16,8,256]{2,1,0:T(8,128)} %sp.1) | copy-start | bytes 393220
  12.8 2.4 %collective-permute-start.3 = (bf16[2,2,8,16,256]{4,3,2,1,0:T(8,128)(2,1)S(1)}, bf16[2,2,8,16,256]{4,3,2,1,0:T(8,128)(2,1)S(1)}, u32[]{:S(2)}, u32[]{:S(2)}) collective-permute-start(bf16[2,2,8,16,256]{4,3,2,1,0:T(8,128)(2,1)S(1)} %shard_map.138.own), channel_id=1, source_target_pairs={{0,1},{1,0},{2,3},{3,2},{4,5},{5,4},{6,7},{7,6},{8,9},{9,8},{10,11... | collective-permute-start | bytes 786440 | tf_op jit(solution)/shard_map/ppermute | solution.py:528
  14.0 10.0 %collective-permute-start.2 = (bf16[2,2,8,16,256]{4,3,2,1,0:T(8,128)(2,1)S(1)}, bf16[2,2,8,16,256]{4,3,2,1,0:T(8,128)(2,1)S(1)}, u32[]{:S(2)}, u32[]{:S(2)}) collective-permute-start(bf16[2,2,8,16,256]{4,3,2,1,0:T(8,128)(2,1)S(1)} %shard_map.138.own), channel_id=1, source_target_pairs={{0,15},{1,2},{2,1},{3,4},{4,3},{5,6},{6,5},{7,8},{8,7},{9,10},{10,... | collective-permute-start | bytes 786440 | tf_op jit(solution)/shard_map/ppermute | solution.py:528
  15.2 13.1 %collective-permute-start.4 = (bf16[2,2,8,16,256]{4,3,2,1,0:T(8,128)(2,1)S(1)}, bf16[2,2,8,16,256]{4,3,2,1,0:T(8,128)(2,1)S(1)}, u32[]{:S(2)}, u32[]{:S(2)}) collective-permute-start(bf16[2,2,8,16,256]{4,3,2,1,0:T(8,128)(2,1)S(1)} %collective-permute-done.3.chip), channel_id=1, source_target_pairs={{0,15},{1,2},{2,1},{3,4},{4,3},{5,6},{6,5},{7,8},{8,7},{9,10},{10,... | collective-permute-start | bytes 786440 | tf_op jit(solution)/shard_map/ppermute | solution.py:528
  24.0 4.2 %collective-permute-start.5 = (bf16[2,2,8,16,256]{4,3,2,1,0:T(8,128)(2,1)S(1)}, bf16[2,2,8,16,256]{4,3,2,1,0:T(8,128)(2,1)S(1)}, u32[]{:S(2)}, u32[]{:S(2)}) collective-permute-start(bf16[2,2,8,16,256]{4,3,2,1,0:T(8,128)(2,1)S(1)} %collective-permute-done.2.near), channel_id=1, source_target_pairs={{0,1},{1,0},{2,3},{3,2},{4,5},{5,4},{6,7},{7,6},{8,9},{9,8},{10,11... | collective-permute-start | bytes 786440 | tf_op jit(solution)/shard_map/ppermute | solution.py:528

commit v3 on v2

--- a/solution.py
+++ b/solution.py
@@ -34,13 +34,13 @@
     return copies
 
 
-def call(kernel, outs, in_specs, scratch, mib, flops, bytes_moved, place=VMEM):
-    multiple = isinstance(outs, (list, tuple))
+def call(kernel, outs, in_specs, scratch, mib, flops, bytes_moved, places=None, aliases=None):
     return pl.pallas_call(
         kernel,
         out_shape=outs,
         in_specs=in_specs,
-        out_specs=[place] * len(outs) if multiple else place,
+        out_specs=places or [VMEM] * len(outs),
+        input_output_aliases=aliases or {},
         scratch_shapes=scratch,
         compiler_params=pltpu.CompilerParams(vmem_limit_bytes=mib << 20),
         cost_estimate=pl.CostEstimate(
@@ -126,8 +126,11 @@
 
 
 def pack_kernel(*refs):
-    sources, (out_x, out_s, partial, flat_factor, tilt_factor), rest = refs[:7], refs[7:12], refs[12:]
-    (sn, rn, sb, rb, sp, an, ti, slope, base), sems = rest[:9], rest[9]
+    sources, (out_x, out_s, now, sp, partial, flat_factor, tilt_factor), rest = (
+        refs[:7], refs[7:14], refs[14:],
+    )
+    (sb, rb, an, ti, slope, base), sems = rest[:6], rest[6]
+    sn, rn = now.at[0], now.at[1]
     depth, rows, width = sp.shape
     half = rows // 2
     full = depth * rows
@@ -135,11 +138,12 @@
     row = sublane((rows, LANES))
     lane = lax.broadcasted_iota(jnp.int32, (rows, LANES), 1)
     order = (0, 2, 1, 3, 4, 5, 6)
-    chunk = depth // 2
+    chunks = 4
+    chunk = depth // chunks
     inner = pl.ds(REACH, depth)
     targets = (sn.at[inner], rn.at[inner], sb, rb, sp, an, ti)
     copies = []
-    for c in range(2):
+    for c in range(chunks):
         span = pl.ds(c * chunk, chunk)
         copies.append(
             fetch(
@@ -157,8 +161,8 @@
         factor = sp[z] * (1.0 + 2.0 * an[z])
         flat_factor[z] = factor
         tilt_factor[z] = sp[z] * ti[z]
-        for m, (now, before) in enumerate(((sn, sb), (rn, rb))):
-            value = now[z + REACH]
+        for m, before in enumerate((sb, rb)):
+            value = now[m, z + REACH]
             second, first = flat_terms(value, None, row, lane)
             for p in range(width // LANES):
                 lanes = slice(p * LANES, (p + 1) * LANES)
@@ -168,21 +172,23 @@
                 )
         return c
 
-    for c in range(2):
-        for copy in copies[c]:
-            copy.wait()
-        lax.fori_loop(c * chunk, (c + 1) * chunk, flat, 0, unroll=2)
-
     def deep(z, c):
-        for m, now in enumerate((sn, rn)):
+        for m in range(2):
             partial[m, z] = (
                 base[m, z]
-                + sp[z] * depth_second(now, z)
+                + sp[z] * depth_second(now.at[m], z)
                 + tilt_factor[z] * depth_first(slope.at[m], z)
             )
         return c
 
-    lax.fori_loop(0, depth, deep, 0, unroll=2)
+    for c in range(chunks):
+        for copy in copies[c]:
+            copy.wait()
+        lax.fori_loop(c * chunk, (c + 1) * chunk, flat, 0, unroll=4)
+        done = (c + 1) * chunk if c == chunks - 1 else max((c + 1) * chunk - REACH, 0)
+        start = max(c * chunk - REACH, 0)
+        if done > start:
+            lax.fori_loop(start, done, deep, 0, unroll=4)
     first_half = sublane((depth, rows, width)) < half
 
     def joined(a, b, place):
@@ -193,14 +199,14 @@
         out_x[place * full : (place + 1) * full] = jnp.where(odd, high, low)
         out_s[place * full : (place + 1) * full] = jnp.where(odd, low, high)
 
-    joined(sn[REACH : REACH + depth], rn[REACH : REACH + depth], 0)
+    joined(now[0, REACH : REACH + depth], now[1, REACH : REACH + depth], 0)
     joined(partial[0], partial[1], 1)
     joined(flat_factor[...], tilt_factor[...], 2)
 
 
 def inject_kernel(grid_rows, *refs):
     sources, now, (inj, bins_y, table, edge_flat, edge_slope), held, (onehot, left, sems) = (
-        refs[:6], refs[6:8], refs[8:13], refs[13:19], refs[19:],
+        refs[:6], refs[6], refs[7:12], refs[12:18], refs[18:],
     )
     rc, rt, sc, sw, bins, weights = held
     copies = fetch(sources, held, sems)
@@ -275,7 +281,7 @@
         clear_ends(edge_slope.at[m])
 
         def edge(z, c, m=m):
-            second, first = cross_terms(now[m][z], row, sign)
+            second, first = cross_terms(now[m, z + REACH], row, sign)
             for p in range(width // LANES):
                 lanes = slice(p * LANES, (p + 1) * LANES)
                 edge_flat[m, z, :, lanes] = second[p]
@@ -286,10 +292,11 @@
 
 
 def step_kernel(
-    sn, rn, sp, partial, flat_factor, tilt_factor, edge_flat, edge_slope, px, ps, inj, out,
+    now, sp, partial, flat_factor, tilt_factor, edge_flat, edge_slope, px, ps, inj,
+    out, slim, known,
     slope, base, edge_base, edge_tilt, later, later_edge, turned,
 ):
-    depth, rows, width = sn.shape
+    depth, rows, width = sp.shape
     half = rows // 2
     full = depth * rows
     odd = is_odd()
@@ -297,7 +304,6 @@
     lane = lax.broadcasted_iota(jnp.int32, (rows, LANES), 1)
     sign = jnp.where(row < half, -1.0, 1.0)
     low_half = sublane((rows, width)) < half
-    now = (sn, rn)
     parts = [slice(x, x + LANES) for x in range(0, width, LANES)]
     for m in range(2):
         clear_ends(slope.at[m])
@@ -332,7 +338,7 @@
                     )
         return c
 
-    lax.fori_loop(0, depth // 2, flat, 0)
+    lax.fori_loop(0, depth // 2, flat, 0, unroll=2)
 
     def deep(z, c):
         for m in range(2):
@@ -340,7 +346,7 @@
             later_edge[m, z] = edge_base[m, z] + edge_tilt[z] * depth_first(edge_slope.at[m], z)
         return c
 
-    lax.fori_loop(0, depth, deep, 0, unroll=2)
+    lax.fori_loop(0, depth, deep, 0, unroll=4)
     for m in range(2):
         later[m, REACH] = later[m, REACH] + inj[0, m]
         later_edge[m, 0] = later_edge[m, 0] + inj[1, m]
@@ -353,13 +359,14 @@
                 slope[m, z + REACH, :, lanes] = first[p]
                 base[m, z, :, lanes] = (
                     2.0 * mid[:, lanes]
-                    - now[m][z, :, lanes]
+                    - now[m, z + REACH, :, lanes]
                     + flat_factor[z, :, lanes] * second[p]
                 )
                 turned[0, m, p, pl.ds(z, rows, stride=depth), :] = mid[:, lanes]
+                turned[2, m, p, pl.ds(z, rows, stride=depth), :] = later_edge[m, z, :, lanes]
         return c
 
-    lax.fori_loop(0, depth, flat_later, 0, unroll=2)
+    lax.fori_loop(0, depth, flat_later, 0, unroll=4)
 
     def deep_later(z, c):
         surface = jnp.where(z == 0, 1.0, 0.0)
@@ -374,14 +381,20 @@
                 turned[1, m, p, pl.ds(z, rows, stride=depth), :] = value[:, lanes]
         return c
 
-    lax.fori_loop(0, depth, deep_later, 0, unroll=2)
-    for s in range(STEPS):
-        for m in range(2):
-            for p, lanes in enumerate(parts):
-                for y in range(rows):
-                    out[s, m, y, :, lanes] = turned[
-                        s, m, p, y * depth : (y + 1) * depth, :
-                    ].astype(BF16)
+    lax.fori_loop(0, depth, deep_later, 0, unroll=4)
+    kept = jnp.where(odd, 0, half)
+    for m in range(2):
+        for p, lanes in enumerate(parts):
+            for y in range(rows):
+                plane = slice(y * depth, (y + 1) * depth)
+                out[0, m, y, :, lanes] = turned[0, m, p, plane, :].astype(BF16)
+                last = turned[1, m, p, plane, :].astype(BF16)
+                out[1, m, y, :, lanes] = last
+                slim[(m + 1) * rows + y, :, lanes] = last
+            for y in range(half):
+                plane = pl.ds(pl.multiple_of((kept + y) * depth, depth), depth)
+                slim[m * half + y, :, lanes] = turned[0, m, p, plane, :].astype(BF16)
+                known[m, y, :, lanes] = turned[2, m, p, plane, :].astype(BF16)
 
 
 GROUP = 4
@@ -402,17 +415,20 @@
     return count
 
 
-def add_lags(window, table, ids, picks, groups, y, rows, tiles, sums):
+PAIR = 2
+
+
+def add_lags(window, table, ids, picks, groups, rows, spots, sums):
     steps = window.shape[0]
     angles = table.shape[1]
-    at = y + rows * 2
 
     def one_group(group, sums):
         sums = [list(a) for a in sums]
         for member in range(GROUP):
             lag = picks[0, group * GROUP + member]
             h = picks[1, group * GROUP + member]
-            for n, (z, x) in enumerate(tiles):
+            for n, (y, z, x) in enumerate(spots):
+                at = y + 2 * rows
                 zs, xs = slice(z, z + 8), slice(x, x + LANES)
                 product = None
                 for s in range(steps):
@@ -428,22 +444,37 @@
     return lax.fori_loop(0, groups, one_group, sums)
 
 
-def place_pieces(window, pieces, rows):
-    odd = jnp.where(is_odd(), 1, 0)
-    for piece, place in pieces:
-        block = (place + odd * (4 - 2 * place)) * rows
-        for s in range(STEPS):
-            for m in range(2):
-                window[s, m, pl.ds(block, rows)] = piece[s, m].astype(F32)
+def block_of(place):
+    return place + jnp.where(is_odd(), 4 - 2 * place, 0)
+
+
+def place_whole(window, piece, place, rows):
+    for s in range(STEPS):
+        for m in range(2):
+            window[s, m, pl.ds(block_of(place) * rows, rows)] = piece[s, m].astype(F32)
+
+
+def place_slim(window, slim, known, place, kept, rows):
+    half = rows // 2
+    start = block_of(place) * rows
+    for m in range(2):
+        window[0, m, pl.ds(start + kept, half)] = known[m].astype(F32)
+        window[0, m, pl.ds(start + half - kept, half)] = slim[
+            m * half : (m + 1) * half
+        ].astype(F32)
+        window[1, m, pl.ds(start, rows)] = slim[(m + 1) * rows : (m + 2) * rows].astype(F32)
 
 
 def near_image_kernel(
-    lags_in, near, own, chip, bins, table, out, far_picks, window, lags, picks, sems
+    lags_in, near, known, own, chip, bins, table, out, far_picks, window, lags, picks, sems
 ):
     copies = fetch([lags_in], [lags], sems)
     rows, depth, width = bins.shape
     angles = table.shape[1]
-    place_pieces(window, ((near, 1), (own, 2), (chip, 3)), rows)
+    kept = jnp.where(is_odd(), 0, rows // 2)
+    place_slim(window, near, known, 1, kept, rows)
+    place_whole(window, own, 2, rows)
+    place_whole(window, chip, 3, rows)
     copies[0].wait()
     count = listed(lags, rows, False, picks)
     row = lax.broadcasted_iota(jnp.int32, far_picks.shape, 0)
@@ -460,8 +491,9 @@
 
     def one_row(y, c):
         ids = [bins[y, z : z + 8, x : x + LANES] for z, x in tiles]
+        spots = [(y, z, x) for z, x in tiles]
         sums = tuple((zero,) * len(tiles) for _ in range(angles))
-        sums = add_lags(window, table, ids, picks, groups, y, rows, tiles, sums)
+        sums = add_lags(window, table, ids, picks, groups, rows, spots, sums)
         for a in range(angles):
             for n, (z, x) in enumerate(tiles):
                 out[a, y, z : z + 8, x : x + LANES] = sums[a][n]
@@ -471,38 +503,44 @@
 
 
 def far_image_kernel(
-    before, picks_in, far, near, own, chip, relay, bins, table, out,
-    window, turned, staged, picks, sems,
+    before, picks_in, window_in, far, relay, hint, bins, table, out, window,
+    turned, staged, picks, sems,
 ):
-    pick = pltpu.make_async_copy(picks_in, picks, sems.at[0])
-    pick.start()
+    del window_in
     rows, depth, width = bins.shape
     angles = table.shape[1]
-    place_pieces(window, ((far, 0), (near, 1), (own, 2), (chip, 3), (relay, 4)), rows)
-    pick.wait()
-    groups = lax.div(picks[2, 0] + (GROUP - 1), GROUP)
+    half = rows // 2
+    for n in range(table.shape[0] - 1 + GROUP):
+        picks[0, n] = picks_in[0, n]
+        picks[1, n] = picks_in[1, n]
+    groups = lax.div(picks_in[2, 0] + (GROUP - 1), GROUP)
+    place_whole(window, far, 0, rows)
+    place_slim(window, relay, hint, 4, jnp.where(is_odd(), half, 0), rows)
     sends = []
-    for part in range(width // LANES):
-        lanes = slice(part * LANES, (part + 1) * LANES)
-        tiles = [(z, part * LANES) for z in range(0, depth, 8)]
-
-        def one_row(y, c, tiles=tiles, lanes=lanes):
-            ids = [bins[y, z : z + 8, lanes] for z, _ in tiles]
+    for piece in range(depth // 8):
+        zs = slice(piece * 8, (piece + 1) * 8)
+        tiles = [(piece * 8, x) for x in range(0, width, LANES)]
+
+        def some_rows(pair, c, tiles=tiles):
+            spots = [(PAIR * pair + r, z, x) for r in range(PAIR) for z, x in tiles]
+            ids = [bins[y, z : z + 8, x : x + LANES] for y, z, x in spots]
             sums = tuple(
-                tuple(before[a, y, z : z + 8, lanes] for z, _ in tiles) for a in range(angles)
+                tuple(before[a, y, z : z + 8, x : x + LANES] for y, z, x in spots)
+                for a in range(angles)
             )
-            sums = add_lags(window, table, ids, picks, groups, y, rows, tiles, sums)
+            sums = add_lags(window, table, ids, picks, groups, rows, spots, sums)
             for a in range(angles):
-                for n, (z, _) in enumerate(tiles):
-                    turned[a, pl.ds(z * rows + y, 8, stride=rows), :] = sums[a][n]
+                for n, (y, z, x) in enumerate(spots):
+                    turned[a, x // LANES, pl.ds(y, 8, stride=rows), :] = sums[a][n]
             return c
 
-        lax.fori_loop(0, rows, one_row, 0)
+        lax.fori_loop(0, rows // PAIR, some_rows, 0)
         for a in range(angles):
-            staged[part, a] = turned[a].astype(BF16).reshape(depth, rows, LANES)
-        send = pltpu.make_async_copy(
-            staged.at[part], out.at[:, :, :, lanes], sems.at[1 + part]
-        )
+            for n, (_, x) in enumerate(tiles):
+                staged[piece, a, :, :, x : x + LANES] = (
+                    turned[a, n].astype(BF16).reshape(8, rows, LANES)
+                )
+        send = pltpu.make_async_copy(staged.at[piece], out.at[:, zs], sems.at[1 + piece])
         send.start()
         sends.append(send)
     for send in sends:
@@ -534,22 +572,23 @@
     tall = depth + 2 * REACH
     grid = (depth, rows, width)
     pack_shape = jax.ShapeDtypeStruct((3 * full, width), BF16)
-    pack_x, pack_s, partial, flat_factor, tilt_factor = call(
+    pack_x, pack_s, now, speed, partial, flat_factor, tilt_factor = call(
         pack_kernel,
         [
             pack_shape,
             pack_shape,
+            jax.ShapeDtypeStruct((2, tall, rows, width), F32),
+            jax.ShapeDtypeStruct(grid, F32),
             jax.ShapeDtypeStruct((2,) + grid, F32),
             jax.ShapeDtypeStruct(grid, F32),
             jax.ShapeDtypeStruct(grid, F32),
         ],
         [HBM] * 7,
-        [pltpu.VMEM((tall, rows, width), F32)] * 2
-        + [pltpu.VMEM(grid, F32)] * 5
+        [pltpu.VMEM(grid, F32)] * 4
         + [
             pltpu.VMEM((2, tall, rows, width), F32),
             pltpu.VMEM((2,) + grid, F32),
-            pltpu.SemaphoreType.DMA((2, 7)),
+            pltpu.SemaphoreType.DMA((4, 7)),
         ],
         8,
         full * width * 200,
@@ -567,7 +606,7 @@
             jax.ShapeDtypeStruct((2,) + grid, F32),
             jax.ShapeDtypeStruct((2, tall, rows, width), F32),
         ],
-        [HBM] * 6 + [VMEM] * 2,
+        [HBM] * 6 + [VMEM],
         [
             pltpu.VMEM((1, count), jnp.int32),
             pltpu.VMEM((STEPS, count), F32),
@@ -593,14 +632,18 @@
                 jnp.transpose(weight_table, (1, 2, 0)),
             )
         ),
-        source_now,
-        receiver_now,
-    )
-
-    own = call(
+        now,
+    )
+
+    half = rows // 2
+    own, slim, known = call(
         step_kernel,
-        jax.ShapeDtypeStruct((STEPS, 2, rows, depth, width), BF16),
-        [VMEM] * 11,
+        [
+            jax.ShapeDtypeStruct((STEPS, 2, rows, depth, width), BF16),
+            jax.ShapeDtypeStruct((2 * (half + rows), depth, width), BF16),
+            jax.ShapeDtypeStruct((2, half, depth, width), BF16),
+        ],
+        [VMEM] * 10,
         [
             pltpu.VMEM((2, tall, rows, width), F32),
             pltpu.VMEM((2,) + grid, F32),
@@ -608,31 +651,31 @@
             pltpu.VMEM(grid, F32),
             pltpu.VMEM((2, tall, rows, width), F32),
             pltpu.VMEM((2,) + grid, F32),
-            pltpu.VMEM((STEPS, 2, parts, full, LANES), F32),
+            pltpu.VMEM((STEPS + 1, 2, parts, full, LANES), F32),
         ],
         16,
         full * width * 300,
         full * width * 50,
     )(
-        source_now, receiver_now, speed_term, partial, flat_factor, tilt_factor, edge_flat,
-        edge_slope, got_x, got_s, inj,
+        now, speed, partial, flat_factor, tilt_factor, edge_flat, edge_slope, got_x, got_s, inj,
     )
 
     chip = moved(own, chip_route)
-    near = moved(own, near_route)
+    near = moved(slim, near_route)
     far = moved(chip, near_route)
+    hint = moved(known, chip_route)
     relay = moved(near, chip_route)
-    window = pltpu.VMEM((STEPS, 2, 5 * rows, depth, width), F32)
+    window_shape = jax.ShapeDtypeStruct((STEPS, 2, 5 * rows, depth, width), F32)
     pick_space = pltpu.SMEM((8, LANES), jnp.int32)
-    half_image, far_picks = call(
+    half_image, far_picks, window = call(
         near_image_kernel,
         [
             jax.ShapeDtypeStruct((angles, rows, depth, width), F32),
             jax.ShapeDtypeStruct((8, LANES), jnp.int32),
-        ],
-        [HBM] + [VMEM] * 5,
+            window_shape,
+        ],
+        [HBM] + [VMEM] * 6,
         [
-            window,
             pltpu.SMEM(offset_lags.shape, jnp.int32),
             pick_space,
             pltpu.SemaphoreType.DMA((1,)),
@@ -640,23 +683,24 @@
         16,
         full * width * lag_count * 6,
         full * width * 20,
-    )(*in_hbm((offset_lags,)), near, own, chip, bins_y, table)
+    )(*in_hbm((offset_lags,)), near, known, own, chip, bins_y, table)
+    pieces = depth // 8
     return call(
         far_image_kernel,
-        jax.ShapeDtypeStruct((angles, depth, rows, width), BF16),
-        [VMEM] * 9,
+        [jax.ShapeDtypeStruct((angles, depth, rows, width), BF16), window_shape],
+        [VMEM] * 8,
         [
-            window,
-            pltpu.VMEM((angles, full, LANES), F32),
-            pltpu.VMEM((parts, angles, depth, rows, LANES), BF16),
+            pltpu.VMEM((angles, parts, 8 * rows, LANES), F32),
+            pltpu.VMEM((pieces, angles, 8, rows, width), BF16),
             pick_space,
-            pltpu.SemaphoreType.DMA((1 + parts,)),
+            pltpu.SemaphoreType.DMA((1 + pieces,)),
         ],
         16,
         full * width * lag_count * 6,
         full * width * 20,
-        HBM,
-    )(half_image, far_picks, far, near, own, chip, relay, bins_y, table)
+        [HBM, VMEM],
+        {2: 1},
+    )(half_image, far_picks, window, far, relay, hint, bins_y, table)[0]
 
 
 def solution(mesh):

time: 31.6 us -> 29.1 us (0.921)
  the two profiles are of different devices: /device:TPU:1 before, /device:TPU:0 now
where the time goes in v3:
time: 29.1 us; the launch traced here: 28.9 us
  starting transfers between devices  12.7 us (44%)
  Pallas kernels  11 us (38%)
  waiting for transfers between devices  5.07 us (17%)
    ppermute x7, starting transfers between devices, moved(): return lax.ppermute(block, 'gy', route)  12.7 us
    ppermute x7, waiting for transfers between devices, moved(): return lax.ppermute(block, 'gy', route)  5.07 us
    pallas_call x1, Pallas kernels, per_device(): call(far_image_kernel, [jax.ShapeDtypeStruct((angles, depth, rows, width)...  2.42 us
    pallas_call x1, Pallas kernels, per_device(): call(pack_kernel, [pack_shape, pack_shape, jax.ShapeDtypeStruct((2, tall,...  2.27 us
    pallas_call x1, Pallas kernels, per_device(): call(functools.partial(inject_kernel, size * rows), [jax.ShapeDtypeStruct...  2.15 us
    pallas_call x1, Pallas kernels, per_device(): call(near_image_kernel, [jax.ShapeDtypeStruct((angles, rows, depth, width...  2.13 us
    pallas_call x1, Pallas kernels, per_device(): call(step_kernel, [jax.ShapeDtypeStruct((STEPS, 2, rows, depth, width), B...  2.09 us
  transfers between devices with their start and end apart: 7, of which 3 were waited for; matrix products, arithmetic and copies ran while one was open for 0% of the time, Pallas kernels for 15%

profile of v3, /device:TPU:0, one launch (start us, length us, event | category | flops | bytes accessed | tf_op | source)
XLA Modules:
  0.0 28.9 jit_solution(1106159507786172636)
XLA Ops:
  0.0 2.3 %shard_map.136 = (bf16[384,256]{1,0:T(8,128)(2,1)S(1)}, bf16[384,256]{1,0:T(8,128)(2,1)S(1)}, f32[2,24,8,256]{3,2,1,0:T(8,128)S(1)}, f32[16,8,256]{2,1,0:T(8,128...) custom-call(f32[16,8,256]{2,1,0:T(8,128)} %refs_0_.1, ...), custom_call_target="tpu_custom_call" | custom-call | flops 6553600 | bytes 1310720 | tf_op jit(solution)/shard_map/pallas_call | solution.py:575
  2.3 5.5 %collective-permute-start = (bf16[384,256]{1,0:T(8,128)(2,1)S(1)}, bf16[384,256]{1,0:T(8,128)(2,1)S(1)}, u32[]{:S(2)}, u32[]{:S(2)}) collective-permute-start(bf16[384,256]{1,0:T(8,128)(2,1)S(1)} %get-tuple-element.31), channel_id=1, source_target_pairs={{0,15},{1,2},{2,1},{3,4},{4,3},{5,6},{6,5},{7,8},{8,7},{9,10},{10,... | collective-permute-start | bytes 589832 | tf_op jit(solution)/shard_map/ppermute | solution.py:566
  7.8 0.0 collective-permute-start.1
  7.8 2.1 %shard_map.137 = (f32[3,2,8,256]{3,2,1,0:T(8,128)S(1)}, s32[8,16,256]{2,1,0:T(8,128)S(1)}, f32[25,4,8,128]{3,2,1,0:T(8,128)S(1)}, f32[2,16,8,256]{3,2,1,0:T(8,128)S(1)}, f32[2,24,8,256]{3,2,1,0:T(8,128)S(1)}) custom-call(s32[1,2048]{1,0:T(1,128)} %bitcast.2, f32[2,2048]{1,0:T(2,128)} %refs_1_.3, s32[8]{0:T(128)} %refs_2_.3, f32[2,8]{1,0:T(2,128)} %refs_3_.3, ...), custom_call_target="tpu_custom_call" | custom-call | flops 50331648 | bytes 262144 | tf_op jit(solution)/shard_map/pallas_call | solution.py:600
  10.0 1.2 %collective-permute-done.px = bf16[384,256]{1,0:T(8,128)(2,1)S(1)} collective-permute-done((bf16[384,256]{1,0:T(8,128)(2,1)S(1)}, bf16[384,256]{1,0:T(8,128)(2,1)S(1)}, u32[]{:S(2)}, u32[]{:S(2)}) %collective-permute-start) | collective-permute-done | bytes 196640 | tf_op jit(solution)/shard_map/ppermute | solution.py:566
  11.2 0.0 collective-permute-done.1.ps
  11.2 2.1 %shard_map.138 = (bf16[2,2,8,16,256]{4,3,2,1,0:T(8,128)(2,1)S(1)}, bf16[24,16,256]{2,1,0:T(8,128)(2,1)S(1)}, bf16[2,4,16,256]{3,2,1,0:T(8,128)(2,1)S(1)}) custom-call(f32[2,24,8,256]{3,2,1,0:T(8,128)S(1)} %get-tuple-element.24.refs_6_.now, f32[16,8,256]{2,1,0:T(8,128)S(1)} %get-tuple-element.25.sp, f32[2,16,8,256]{3,2,1,0:T(8,128)S(1)} %get-tuple-element.26.partial, ...), custom_call_target="tpu_custom_call" | custom-call | flops 9830400 | bytes 1638400 | tf_op jit(solution)/shard_map/pallas_call | solution.py:639
  13.3 0.1 collective-permute-start.3
  13.3 4.5 %collective-permute-start.2 = (bf16[24,16,256]{2,1,0:T(8,128)(2,1)S(1)}, bf16[24,16,256]{2,1,0:T(8,128)(2,1)S(1)}, u32[]{:S(2)}, u32[]{:S(2)}) collective-permute-start(bf16[24,16,256]{2,1,0:T(8,128)(2,1)S(1)} %get-tuple-element.34), channel_id=1, source_target_pairs={{0,15},{1,2},{2,1},{3,4},{4,3},{5,6},{6,5},{7,8},{8,7},{9,10},{10,... | collective-permute-start | bytes 589832 | tf_op jit(solution)/shard_map/ppermute | solution.py:566
  17.8 0.0 collective-permute-done.3.chip
  17.9 1.5 %collective-permute-start.4 = (bf16[2,2,8,16,256]{4,3,2,1,0:T(8,128)(2,1)S(1)}, bf16[2,2,8,16,256]{4,3,2,1,0:T(8,128)(2,1)S(1)}, u32[]{:S(2)}, u32[]{:S(2)}) collective-permute-start(bf16[2,2,8,16,256]{4,3,2,1,0:T(8,128)(2,1)S(1)} %collective-permute-done.3.chip), channel_id=1, source_target_pairs={{0,15},{1,2},{2,1},{3,4},{4,3},{5,6},{6,5},{7,8},{8,7},{9,10},{10,... | collective-permute-start | bytes 786440 | tf_op jit(solution)/shard_map/ppermute | solution.py:566
  19.3 2.0 %collective-permute-done.2.near = bf16[24,16,256]{2,1,0:T(8,128)(2,1)S(1)} collective-permute-done((bf16[24,16,256]{2,1,0:T(8,128)(2,1)S(1)}, bf16[24,16,256]{2,1,0:T(8,128)(2,1)S(1)}, u32[]{:S(2)}, u32[]{:S(2)}) %collective-permute-start.2) | collective-permute-done | bytes 196640 | tf_op jit(solution)/shard_map/ppermute | solution.py:566
  21.3 1.1 %collective-permute-start.5 = (bf16[24,16,256]{2,1,0:T(8,128)(2,1)S(1)}, bf16[24,16,256]{2,1,0:T(8,128)(2,1)S(1)}, u32[]{:S(2)}, u32[]{:S(2)}) collective-permute-start(bf16[24,16,256]{2,1,0:T(8,128)(2,1)S(1)} %collective-permute-done.2.near), channel_id=1, source_target_pairs={{0,1},{1,0},{2,3},{3,2},{4,5},{5,4},{6,7},{7,6},{8,9},{9,8},{10,11... | collective-permute-start | bytes 589832 | tf_op jit(solution)/shard_map/ppermute | solution.py:566
  22.4 0.0 collective-permute-start.6
  22.4 2.1 %shard_map.139 = (f32[4,8,16,256]{3,2,1,0:T(8,128)S(1)}, s32[8,128]{1,0:T(8,128)S(1)}, f32[2,2,40,16,256]{4,3,2,1,0:T(8,128)S(1)}) custom-call(s32[24]{0:T(128)} %lags_in.1, bf16[24,16,256]{2,1,0:T(8,128)(2,1)S(1)} %collective-permute-done.2.near, bf16[2,4,16,256]{3,2,1,0:T(8,128)(2,1)S(1)} %get-tuple-element.35.known, ...), custom_call_target="tpu_custom_call" | custom-call | flops 4718592 | bytes 655360 | tf_op jit(solution)/shard_map/pallas_call | solution.py:670
  24.6 0.0 collective-permute-done.6.hint
  24.6 0.0 collective-permute-done.5.relay
  24.6 1.9 %collective-permute-done.4.far = bf16[2,2,8,16,256]{4,3,2,1,0:T(8,128)(2,1)S(1)} collective-permute-done((bf16[2,2,8,16,256]{4,3,2,1,0:T(8,128)(2,1)S(1)}, bf16[2,2,8,16,256]{4,3,2,1,0:T(8,128)(2,1)S(1)}, u32[]{:S(2)}, u32[]{:S(2)}) %collective-permute-start.4) | collective-permute-done | bytes 262176 | tf_op jit(solution)/shard_map/ppermute | solution.py:566
  26.4 2.4 %shard_map.140 = (bf16[4,16,8,256]{3,2,1,0:T(8,128)(2,1)}, f32[2,2,40,16,256]{4,3,2,1,0:T(8,128)S(1)}) custom-call(f32[4,8,16,256]{3,2,1,0:T(8,128)S(1)} %get-tuple-element.39.before, s32[8,128]{1,0:T(8,128)S(1)} %get-tuple-element.40.picks_in, f32[2,2,40,16,256]{4,3,2,1,0:T(8,128)S(1)} %get-tuple-element.41.window_in, ...), custom_call_target="tpu_custom_call", output_to_operand_aliasing={{1}: (2, {})} | custom-call | flops 4718592 | bytes 655360 | tf_op jit(solution)/shard_map/pallas_call | solution.py:688
Async XLA Ops:
  2.3 8.9 %collective-permute-start = (bf16[384,256]{1,0:T(8,128)(2,1)S(1)}, bf16[384,256]{1,0:T(8,128)(2,1)S(1)}, u32[]{:S(2)}, u32[]{:S(2)}) collective-permute-start(bf16[384,256]{1,0:T(8,128)(2,1)S(1)} %get-tuple-element.31), channel_id=1, source_target_pairs={{0,15},{1,2},{2,1},{3,4},{4,3},{5,6},{6,5},{7,8},{8,7},{9,10},{10,... | collective-permute-start | bytes 589832 | tf_op jit(solution)/shard_map/ppermute | solution.py:566
  7.8 3.4 %collective-permute-start.1 = (bf16[384,256]{1,0:T(8,128)(2,1)S(1)}, bf16[384,256]{1,0:T(8,128)(2,1)S(1)}, u32[]{:S(2)}, u32[]{:S(2)}) collective-permute-start(bf16[384,256]{1,0:T(8,128)(2,1)S(1)} %get-tuple-element.32), channel_id=1, source_target_pairs={{0,1},{1,0},{2,3},{3,2},{4,5},{5,4},{6,7},{7,6},{8,9},{9,8},{10,11... | collective-permute-start | bytes 589832 | tf_op jit(solution)/shard_map/ppermute | solution.py:566
  13.3 4.6 %collective-permute-start.3 = (bf16[2,2,8,16,256]{4,3,2,1,0:T(8,128)(2,1)S(1)}, bf16[2,2,8,16,256]{4,3,2,1,0:T(8,128)(2,1)S(1)}, u32[]{:S(2)}, u32[]{:S(2)}) collective-permute-start(bf16[2,2,8,16,256]{4,3,2,1,0:T(8,128)(2,1)S(1)} %get-tuple-element.36.own), channel_id=1, source_target_pairs={{0,1},{1,0},{2,3},{3,2},{4,5},{5,4},{6,7},{7,6},{8,9},{9,8},{10,11... | collective-permute-start | bytes 786440 | tf_op jit(solution)/shard_map/ppermute | solution.py:566
  13.3 8.0 %collective-permute-start.2 = (bf16[24,16,256]{2,1,0:T(8,128)(2,1)S(1)}, bf16[24,16,256]{2,1,0:T(8,128)(2,1)S(1)}, u32[]{:S(2)}, u32[]{:S(2)}) collective-permute-start(bf16[24,16,256]{2,1,0:T(8,128)(2,1)S(1)} %get-tuple-element.34), channel_id=1, source_target_pairs={{0,15},{1,2},{2,1},{3,4},{4,3},{5,6},{6,5},{7,8},{8,7},{9,10},{10,... | collective-permute-start | bytes 589832 | tf_op jit(solution)/shard_map/ppermute | solution.py:566
  17.9 8.6 %collective-permute-start.4 = (bf16[2,2,8,16,256]{4,3,2,1,0:T(8,128)(2,1)S(1)}, bf16[2,2,8,16,256]{4,3,2,1,0:T(8,128)(2,1)S(1)}, u32[]{:S(2)}, u32[]{:S(2)}) collective-permute-start(bf16[2,2,8,16,256]{4,3,2,1,0:T(8,128)(2,1)S(1)} %collective-permute-done.3.chip), channel_id=1, source_target_pairs={{0,15},{1,2},{2,1},{3,4},{4,3},{5,6},{6,5},{7,8},{8,7},{9,10},{10,... | collective-permute-start | bytes 786440 | tf_op jit(solution)/shard_map/ppermute | solution.py:566
  21.3 3.3 %collective-permute-start.5 = (bf16[24,16,256]{2,1,0:T(8,128)(2,1)S(1)}, bf16[24,16,256]{2,1,0:T(8,128)(2,1)S(1)}, u32[]{:S(2)}, u32[]{:S(2)}) collective-permute-start(bf16[24,16,256]{2,1,0:T(8,128)(2,1)S(1)} %collective-permute-done.2.near), channel_id=1, source_target_pairs={{0,1},{1,0},{2,3},{3,2},{4,5},{5,4},{6,7},{7,6},{8,9},{9,8},{10,11... | collective-permute-start | bytes 589832 | tf_op jit(solution)/shard_map/ppermute | solution.py:566
  22.4 2.1 %collective-permute-start.6 = (bf16[2,4,16,256]{3,2,1,0:T(8,128)(2,1)S(1)}, bf16[2,4,16,256]{3,2,1,0:T(8,128)(2,1)S(1)}, u32[]{:S(2)}, u32[]{:S(2)}) collective-permute-start(bf16[2,4,16,256]{3,2,1,0:T(8,128)(2,1)S(1)} %get-tuple-element.35.known), channel_id=1, source_target_pairs={{0,1},{1,0},{2,3},{3,2},{4,5},{5,4},{6,7},{7,6},{8,9},{9,8},{10,11... | collective-permute-start | bytes 196616 | tf_op jit(solution)/shard_map/ppermute | solution.py:566

commit v4 on v3

--- a/solution.py
+++ b/solution.py
@@ -81,8 +81,9 @@
             outer_down = 0.0 if edges is None else row_roll(edges[p], k)
             up = jnp.where(row < rows - k, row_roll(part, -k), outer_up)
             down = jnp.where(row >= k, row_roll(part, k), outer_down)
-            second[p] = second[p] + SECOND[k] * ((above + below) + (up + down))
-            term = FIRST[k - 1] * ((above - below) + (up - down))
+            ahead, behind = above + up, below + down
+            second[p] = second[p] + SECOND[k] * (ahead + behind)
+            term = FIRST[k - 1] * (ahead - behind)
             first[p] = term if first[p] is None else first[p] + term
     return second, first
 
@@ -205,13 +206,13 @@
 
 
 def inject_kernel(grid_rows, *refs):
-    sources, now, (inj, bins_y, table, edge_flat, edge_slope), held, (onehot, left, sems) = (
-        refs[:6], refs[6], refs[7:12], refs[12:18], refs[18:],
-    )
-    rc, rt, sc, sw, bins, weights = held
+    sources, now, (inj, edge_flat, edge_slope), held, (onehot, left, sems) = (
+        refs[:4], refs[4], refs[5:8], refs[8:12], refs[12:],
+    )
+    rc, rt, sc, sw = held
     copies = fetch(sources, held, sems)
     count = rc.shape[1]
-    depth, rows, width = bins.shape
+    depth, rows, width = edge_flat.shape[1:]
     first_row = lax.axis_index("gy") * rows
     half = rows // 2
     shift = width.bit_length() - 1
@@ -231,12 +232,18 @@
 
     copies[0].wait()
     copies[1].wait()
+    exact = width <= 256
+    columns = lax.broadcasted_iota(jnp.int32, (width, LANES), 0)
+    if exact:
+        columns = columns.astype(F32).astype(BF16)
+    one, none = (jnp.ones((), BF16), jnp.zeros((), BF16)) if exact else (1.0, 0.0)
     for start in range(0, count, LANES):
         cells = rc[:, start : start + LANES]
         at_row = row_of(cells)
         at_col = cells - at_row * width
-        cols = lax.broadcasted_iota(jnp.int32, (width, LANES), 0)
-        onehot[:, start : start + LANES] = jnp.where(cols == at_col, 1.0, 0.0).astype(BF16)
+        if exact:
+            at_col = at_col.astype(F32).astype(BF16)
+        onehot[:, start : start + LANES] = jnp.where(columns == at_col, one, none).astype(BF16)
         parts = []
         for step, wanted in ((0, own_row), (0, edge_row), (1, own_row)):
             amount = rt[step : step + 1, start : start + LANES]
@@ -263,10 +270,86 @@
             here = jnp.logical_and(wanted == at_row, cols == at_col)
             total = total + jnp.where(here, sw[step, i], 0.0)
         inj[place, 0] = total
-    copies[4].wait()
+    row = sublane((rows, LANES))
+    sign = jnp.where(row < half, -1.0, 1.0)
+    for m in range(2):
+        clear_ends(edge_slope.at[m])
+
+        def edge(z, c, m=m):
+            second, first = cross_terms(now[m, z + REACH], row, sign)
+            for p in range(width // LANES):
+                lanes = slice(p * LANES, (p + 1) * LANES)
+                edge_flat[m, z, :, lanes] = second[p]
+                edge_slope[m, z + REACH, :, lanes] = first[p]
+            return c
+
+        lax.fori_loop(0, depth, edge, 0, unroll=2)
+
+
+GROUP = 4
+
+
+def listed(lags, rows, picks):
+    count = jnp.int32(0)
+    total = lags.shape[0]
+    for h in range(total):
+        lag = lags[h]
+        inside = jnp.logical_and(lag <= rows, lag >= -rows)
+        picks[0, count] = lag
+        picks[1, count] = h
+        count = count + jnp.where(inside, 1, 0)
+    for n in range(GROUP):
+        picks[0, count + n] = 0
+        picks[1, count + n] = total
+    return count
+
+
+def list_rows(counts, picks, entries, shape):
+    row = lax.broadcasted_iota(jnp.int32, shape, 0)
+    lane = lax.broadcasted_iota(jnp.int32, shape, 1)
+    held = jnp.zeros(shape, jnp.int32)
+    for n, count in enumerate(counts):
+        held = jnp.where(jnp.logical_and(lane == n, row == 2), count, held)
+    for n in range(entries):
+        value = jnp.where(row == 0, picks[0, n], picks[1, n])
+        held = jnp.where(jnp.logical_and(lane == n, row < 2), value, held)
+    return held
+
+
+def listed_far(lags, rows, picks, counts):
+    count = jnp.int32(0)
+    total = lags.shape[0]
+    counts[0] = count
+    for size in range(rows + 1, 2 * rows + 1):
+        for h in range(total):
+            lag = lags[h]
+            picks[0, count] = lag
+            picks[1, count] = h
+            count = count + jnp.where(jnp.logical_or(lag == size, lag == -size), 1, 0)
+        counts[size - rows] = count
+    for n in range(GROUP):
+        picks[0, count + n] = 0
+        picks[1, count + n] = total
+
+
+def read_list(listed_in, picks, entries, counts=0):
+    for n in range(counts):
+        picks[2, n] = listed_in[2, n]
+    for n in range(entries):
+        picks[0, n] = listed_in[0, n]
+        picks[1, n] = listed_in[1, n]
+
+
+def table_kernel(
+    bins_in, weights_in, lags_in, bins_y, table, near_list, far_list,
+    bins, weights, lags, picks, counts, sems,
+):
+    copies = fetch((bins_in, weights_in, lags_in), (bins, weights, lags), sems)
+    rows = bins.shape[1]
+    copies[0].wait()
     for y in range(rows):
         bins_y[y] = bins[:, y, :]
-    copies[5].wait()
+    copies[1].wait()
     table_rows, angles, bin_count, lanes = table.shape
     lag_count = table_rows - 1
     table[lag_count] = jnp.zeros((angles, bin_count, lanes), F32)
@@ -275,20 +358,13 @@
         slab = values[:, a, :]
         for h in range(lag_count):
             table[h, a] = jnp.broadcast_to(slab[:, h : h + 1], (bin_count, lanes))
-    row = sublane((rows, LANES))
-    sign = jnp.where(row < half, -1.0, 1.0)
-    for m in range(2):
-        clear_ends(edge_slope.at[m])
-
-        def edge(z, c, m=m):
-            second, first = cross_terms(now[m, z + REACH], row, sign)
-            for p in range(width // LANES):
-                lanes = slice(p * LANES, (p + 1) * LANES)
-                edge_flat[m, z, :, lanes] = second[p]
-                edge_slope[m, z + REACH, :, lanes] = first[p]
-            return c
-
-        lax.fori_loop(0, depth, edge, 0, unroll=2)
+    copies[2].wait()
+    count = listed(lags, rows, picks)
+    near_list[...] = list_rows((count,), picks, lag_count + GROUP, near_list.shape)
+    listed_far(lags, rows, picks, counts)
+    far_list[...] = list_rows(
+        [counts[n] for n in range(rows + 1)], picks, lag_count + GROUP, far_list.shape
+    )
 
 
 def step_kernel(
@@ -397,28 +473,11 @@
                 known[m, y, :, lanes] = turned[2, m, p, plane, :].astype(BF16)
 
 
-GROUP = 4
-
-
-def listed(lags, rows, near, picks):
-    count = jnp.int32(0)
-    total = lags.shape[0]
-    for h in range(total):
-        lag = lags[h]
-        inside = jnp.logical_and(lag <= rows, lag >= -rows)
-        picks[0, count] = lag
-        picks[1, count] = h
-        count = count + jnp.where(inside == near, 1, 0)
-    for n in range(GROUP):
-        picks[0, count + n] = 0
-        picks[1, count + n] = total
-    return count
-
-
 PAIR = 2
 
 
 def add_lags(window, table, ids, picks, groups, rows, spots, sums):
+    first, end = groups
     steps = window.shape[0]
     angles = table.shape[1]
 
@@ -441,7 +500,7 @@
                     sums[a][n] = sums[a][n] + weight * product
         return tuple(tuple(a) for a in sums)
 
-    return lax.fori_loop(0, groups, one_group, sums)
+    return lax.fori_loop(first, end, one_group, sums)
 
 
 def block_of(place):
@@ -465,27 +524,15 @@
         window[1, m, pl.ds(start, rows)] = slim[(m + 1) * rows : (m + 2) * rows].astype(F32)
 
 
-def near_image_kernel(
-    lags_in, near, known, own, chip, bins, table, out, far_picks, window, lags, picks, sems
-):
-    copies = fetch([lags_in], [lags], sems)
+def near_image_kernel(near_list, near, known, own, chip, bins, table, out, window, picks):
     rows, depth, width = bins.shape
     angles = table.shape[1]
+    read_list(near_list, picks, table.shape[0] - 1 + GROUP)
+    groups = (0, lax.div(near_list[2, 0] + (GROUP - 1), GROUP))
     kept = jnp.where(is_odd(), 0, rows // 2)
-    place_slim(window, near, known, 1, kept, rows)
     place_whole(window, own, 2, rows)
     place_whole(window, chip, 3, rows)
-    copies[0].wait()
-    count = listed(lags, rows, False, picks)
-    row = lax.broadcasted_iota(jnp.int32, far_picks.shape, 0)
-    lane = lax.broadcasted_iota(jnp.int32, far_picks.shape, 1)
-    held = jnp.where(row == 2, count, 0)
-    for n in range(lags.shape[0] + GROUP):
-        value = jnp.where(row == 0, picks[0, n], picks[1, n])
-        held = jnp.where(jnp.logical_and(lane == n, row < 2), value, held)
-    far_picks[...] = held
-    count = listed(lags, rows, True, picks)
-    groups = lax.div(count + (GROUP - 1), GROUP)
+    place_slim(window, near, known, 1, kept, rows)
     tiles = [(z, x) for z in range(0, depth, 8) for x in range(0, width, LANES)]
     zero = jnp.zeros((8, LANES), F32)
 
@@ -502,45 +549,77 @@
     lax.fori_loop(0, rows, one_row, 0)
 
 
+def early_groups(picks, pair, rows):
+    inside = jnp.where(is_odd(), rows - PAIR - PAIR * pair, PAIR * pair)
+    return lax.div(picks[2, inside], GROUP)
+
+
+def add_pairs(before, window, table, bins, picks, piece, bounds, store):
+    rows, _, width = bins.shape
+    angles = table.shape[1]
+    tiles = [(piece * 8, x) for x in range(0, width, LANES)]
+
+    def some_rows(pair, c):
+        spots = [(PAIR * pair + r, z, x) for r in range(PAIR) for z, x in tiles]
+        ids = [bins[y, z : z + 8, x : x + LANES] for y, z, x in spots]
+        sums = tuple(
+            tuple(before[a, y, z : z + 8, x : x + LANES] for y, z, x in spots)
+            for a in range(angles)
+        )
+        sums = add_lags(window, table, ids, picks, bounds(pair), rows, spots, sums)
+        for a in range(angles):
+            for n, (y, z, x) in enumerate(spots):
+                store(a, y, z, x, sums[a][n])
+        return c
+
+    lax.fori_loop(0, rows // PAIR, some_rows, 0)
+
+
+def mid_image_kernel(
+    before_in, far_list, window_in, relay, hint, bins, table, before, window, picks
+):
+    del before_in, window_in
+    rows, depth, _ = bins.shape
+    read_list(far_list, picks, table.shape[0] - 1 + GROUP, rows + 1)
+    place_slim(window, relay, hint, 4, jnp.where(is_odd(), rows // 2, 0), rows)
+
+    def bounds(pair):
+        return 0, early_groups(picks, pair, rows)
+
+    def store(a, y, z, x, value):
+        before[a, y, z : z + 8, x : x + LANES] = value
+
+    for piece in range(depth // 8):
+        add_pairs(before, window, table, bins, picks, piece, bounds, store)
+
+
 def far_image_kernel(
-    before, picks_in, window_in, far, relay, hint, bins, table, out, window,
-    turned, staged, picks, sems,
+    before, far_list, window_in, far, bins, table, out, window, turned, staged, picks, sems
 ):
     del window_in
     rows, depth, width = bins.shape
     angles = table.shape[1]
-    half = rows // 2
-    for n in range(table.shape[0] - 1 + GROUP):
-        picks[0, n] = picks_in[0, n]
-        picks[1, n] = picks_in[1, n]
-    groups = lax.div(picks_in[2, 0] + (GROUP - 1), GROUP)
+    read_list(far_list, picks, table.shape[0] - 1 + GROUP, rows + 1)
     place_whole(window, far, 0, rows)
-    place_slim(window, relay, hint, 4, jnp.where(is_odd(), half, 0), rows)
+    last = lax.div(picks[2, rows] + (GROUP - 1), GROUP)
+
+    def bounds(pair):
+        return early_groups(picks, pair, rows), last
+
+    def store(a, y, z, x, value):
+        turned[a, x // LANES, pl.ds(y, 8, stride=rows), :] = value
+
     sends = []
     for piece in range(depth // 8):
-        zs = slice(piece * 8, (piece + 1) * 8)
-        tiles = [(piece * 8, x) for x in range(0, width, LANES)]
-
-        def some_rows(pair, c, tiles=tiles):
-            spots = [(PAIR * pair + r, z, x) for r in range(PAIR) for z, x in tiles]
-            ids = [bins[y, z : z + 8, x : x + LANES] for y, z, x in spots]
-            sums = tuple(
-                tuple(before[a, y, z : z + 8, x : x + LANES] for y, z, x in spots)
-                for a in range(angles)
-            )
-            sums = add_lags(window, table, ids, picks, groups, rows, spots, sums)
-            for a in range(angles):
-                for n, (y, z, x) in enumerate(spots):
-                    turned[a, x // LANES, pl.ds(y, 8, stride=rows), :] = sums[a][n]
-            return c
-
-        lax.fori_loop(0, rows // PAIR, some_rows, 0)
+        add_pairs(before, window, table, bins, picks, piece, bounds, store)
         for a in range(angles):
-            for n, (_, x) in enumerate(tiles):
+            for x in range(0, width, LANES):
                 staged[piece, a, :, :, x : x + LANES] = (
-                    turned[a, n].astype(BF16).reshape(8, rows, LANES)
+                    turned[a, x // LANES].astype(BF16).reshape(8, rows, LANES)
                 )
-        send = pltpu.make_async_copy(staged.at[piece], out.at[:, zs], sems.at[1 + piece])
+        send = pltpu.make_async_copy(
+            staged.at[piece], out.at[:, piece * 8 : (piece + 1) * 8], sems.at[piece]
+        )
         send.start()
         sends.append(send)
     for send in sends:
@@ -597,43 +676,52 @@
     got_s = moved(pack_s, chip_route)
     got_x = moved(pack_x, near_route)
 
-    inj, bins_y, table, edge_flat, edge_slope = call(
+    inj, edge_flat, edge_slope = call(
         functools.partial(inject_kernel, size * rows),
         [
             jax.ShapeDtypeStruct((3, 2, rows, width), F32),
-            jax.ShapeDtypeStruct((rows, depth, width), jnp.int32),
-            jax.ShapeDtypeStruct((lag_count + 1, angles, bin_count, LANES), F32),
             jax.ShapeDtypeStruct((2,) + grid, F32),
             jax.ShapeDtypeStruct((2, tall, rows, width), F32),
         ],
-        [HBM] * 6 + [VMEM],
+        [HBM] * 4 + [VMEM],
         [
             pltpu.VMEM((1, count), jnp.int32),
             pltpu.VMEM((STEPS, count), F32),
             pltpu.SMEM(source_cells.shape, jnp.int32),
             pltpu.SMEM(source_wavelet.shape, F32),
-            pltpu.VMEM((depth, rows, width), jnp.int32),
-            pltpu.VMEM((bin_count, angles, lag_count), BF16),
             pltpu.VMEM((width, count), BF16),
             pltpu.VMEM((6 * rows, count), BF16),
-            pltpu.SemaphoreType.DMA((6,)),
+            pltpu.SemaphoreType.DMA((4,)),
         ],
         8,
         12 * rows * count * width,
         full * width * 8,
     )(
-        *in_hbm(
-            (
-                receiver_cells[None],
-                receiver_traces,
-                source_cells,
-                source_wavelet,
-                angle_bins,
-                jnp.transpose(weight_table, (1, 2, 0)),
-            )
-        ),
+        *in_hbm((receiver_cells[None], receiver_traces, source_cells, source_wavelet)),
         now,
     )
+    pick_space = pltpu.SMEM((8, LANES), jnp.int32)
+    bins_y, table, near_list, far_list = call(
+        table_kernel,
+        [
+            jax.ShapeDtypeStruct((rows, depth, width), jnp.int32),
+            jax.ShapeDtypeStruct((lag_count + 1, angles, bin_count, LANES), F32),
+            jax.ShapeDtypeStruct((8, LANES), jnp.int32),
+            jax.ShapeDtypeStruct((8, LANES), jnp.int32),
+        ],
+        [HBM] * 3,
+        [
+            pltpu.VMEM(grid, jnp.int32),
+            pltpu.VMEM((bin_count, angles, lag_count), BF16),
+            pltpu.SMEM(offset_lags.shape, jnp.int32),
+            pick_space,
+            pltpu.SMEM((rows + 1,), jnp.int32),
+            pltpu.SemaphoreType.DMA((3,)),
+        ],
+        8,
+        full * width,
+        full * width * 8,
+    )(*in_hbm((angle_bins, jnp.transpose(weight_table, (1, 2, 0)), offset_lags)))
 
     half = rows // 2
     own, slim, known = call(
@@ -666,41 +754,43 @@
     hint = moved(known, chip_route)
     relay = moved(near, chip_route)
     window_shape = jax.ShapeDtypeStruct((STEPS, 2, 5 * rows, depth, width), F32)
-    pick_space = pltpu.SMEM((8, LANES), jnp.int32)
-    half_image, far_picks, window = call(
+    half_image, window = call(
         near_image_kernel,
-        [
-            jax.ShapeDtypeStruct((angles, rows, depth, width), F32),
-            jax.ShapeDtypeStruct((8, LANES), jnp.int32),
-            window_shape,
-        ],
-        [HBM] + [VMEM] * 6,
-        [
-            pltpu.SMEM(offset_lags.shape, jnp.int32),
-            pick_space,
-            pltpu.SemaphoreType.DMA((1,)),
-        ],
+        [jax.ShapeDtypeStruct((angles, rows, depth, width), F32), window_shape],
+        [VMEM] * 7,
+        [pick_space],
         16,
         full * width * lag_count * 6,
         full * width * 20,
-    )(*in_hbm((offset_lags,)), near, known, own, chip, bins_y, table)
+    )(near_list, near, known, own, chip, bins_y, table)
+    half_image, window = call(
+        mid_image_kernel,
+        [jax.ShapeDtypeStruct((angles, rows, depth, width), F32), window_shape],
+        [VMEM] * 7,
+        [pick_space],
+        16,
+        full * width * lag_count * 3,
+        full * width * 20,
+        None,
+        {0: 0, 2: 1},
+    )(half_image, far_list, window, relay, hint, bins_y, table)
     pieces = depth // 8
     return call(
         far_image_kernel,
         [jax.ShapeDtypeStruct((angles, depth, rows, width), BF16), window_shape],
-        [VMEM] * 8,
+        [VMEM] * 6,
         [
             pltpu.VMEM((angles, parts, 8 * rows, LANES), F32),
             pltpu.VMEM((pieces, angles, 8, rows, width), BF16),
             pick_space,
-            pltpu.SemaphoreType.DMA((1 + pieces,)),
+            pltpu.SemaphoreType.DMA((pieces,)),
         ],
         16,
-        full * width * lag_count * 6,
+        full * width * lag_count * 3,
         full * width * 20,
         [HBM, VMEM],
         {2: 1},
-    )(half_image, far_picks, window, far, relay, hint, bins_y, table)[0]
+    )(half_image, far_list, window, far, bins_y, table)[0]
 
 
 def solution(mesh):

time: 29.1 us -> 29.5 us (1.014)
  the two profiles are of different devices: /device:TPU:0 before, /device:TPU:25 now
where the time goes in v4:
time: 29.5 us; the launch traced here: 29.2 us
  Pallas kernels  12.5 us (42%)
  waiting for transfers between devices  10.9 us (37%)
  starting transfers between devices  5.76 us (20%)
    ppermute x7, waiting for transfers between devices, moved(): return lax.ppermute(block, 'gy', route)  10.9 us
    ppermute x7, starting transfers between devices, moved(): return lax.ppermute(block, 'gy', route)  5.76 us
    pallas_call x1, Pallas kernels, per_device(): call(table_kernel, [jax.ShapeDtypeStruct((rows, depth, width), jnp.int32)...  2.41 us
    pallas_call x1, Pallas kernels, per_device(): call(pack_kernel, [pack_shape, pack_shape, jax.ShapeDtypeStruct((2, tall,...  2.24 us
    pallas_call x1, Pallas kernels, per_device(): call(step_kernel, [jax.ShapeDtypeStruct((STEPS, 2, rows, depth, width), B...  2.08 us
    pallas_call x1, Pallas kernels, per_device(): call(far_image_kernel, [jax.ShapeDtypeStruct((angles, depth, rows, width)...  2.02 us
    pallas_call x1, Pallas kernels, per_device(): call(functools.partial(inject_kernel, size * rows), [jax.ShapeDtypeStruct...  1.64 us
    pallas_call x1, Pallas kernels, per_device(): call(near_image_kernel, [jax.ShapeDtypeStruct((angles, rows, depth, width...  1.31 us
  transfers between devices with their start and end apart: 7, of which 2 were waited for; matrix products, arithmetic and copies ran while one was open for 0% of the time, Pallas kernels for 21%

profile of v4, /device:TPU:25, one launch (start us, length us, event | category | flops | bytes accessed | tf_op | source)
XLA Modules:
  0.0 29.2 jit_solution(803039084506843460)
XLA Ops:
  0.0 2.2 %shard_map.137 = (bf16[384,256]{1,0:T(8,128)(2,1)S(1)}, bf16[384,256]{1,0:T(8,128)(2,1)S(1)}, f32[2,24,8,256]{3,2,1,0:T(8,128)S(1)}, f32[16,8,256]{2,1,0:T(8,128...) custom-call(f32[16,8,256]{2,1,0:T(8,128)} %refs_0_.1, ...), custom_call_target="tpu_custom_call" | custom-call | flops 6553600 | bytes 1310720 | tf_op jit(solution)/shard_map/pallas_call | solution.py:654
  2.2 1.9 %collective-permute-start = (bf16[384,256]{1,0:T(8,128)(2,1)S(1)}, bf16[384,256]{1,0:T(8,128)(2,1)S(1)}, u32[]{:S(2)}, u32[]{:S(2)}) collective-permute-start(bf16[384,256]{1,0:T(8,128)(2,1)S(1)} %get-tuple-element.35), channel_id=1, source_target_pairs={{0,15},{1,2},{2,1},{3,4},{4,3},{5,6},{6,5},{7,8},{8,7},{9,10},{10,... | collective-permute-start | bytes 589832 | tf_op jit(solution)/shard_map/ppermute | solution.py:645
  4.1 0.0 collective-permute-start.1
  4.1 1.6 %shard_map.138 = (f32[3,2,8,256]{3,2,1,0:T(8,128)S(1)}, f32[2,16,8,256]{3,2,1,0:T(8,128)S(1)}, f32[2,24,8,256]{3,2,1,0:T(8,128)S(1)}) custom-call(s32[1,2048]{1,0:T(1,128)} %bitcast.2, f32[2,2048]{1,0:T(2,128)} %refs_1_.3, s32[8]{0:T(128)} %refs_2_.3, f32[2,8]{1,0:T(2,128)} %refs_3_.3, f32[2,24,8,256]{3,2,1,0:T(8,128)S(1)} %get-tuple-element.28.refs_4_.now), custom_call_target="tpu_custom_call" | custom-call | flops 50331648 | bytes 262144 | tf_op jit(solution)/shard_map/pallas_call | solution.py:679
  5.8 3.8 %collective-permute-done.px = bf16[384,256]{1,0:T(8,128)(2,1)S(1)} collective-permute-done((bf16[384,256]{1,0:T(8,128)(2,1)S(1)}, bf16[384,256]{1,0:T(8,128)(2,1)S(1)}, u32[]{:S(2)}, u32[]{:S(2)}) %collective-permute-start) | collective-permute-done | bytes 196640 | tf_op jit(solution)/shard_map/ppermute | solution.py:645
  9.6 0.0 collective-permute-done.1.ps
  9.6 2.1 %shard_map.139 = (bf16[2,2,8,16,256]{4,3,2,1,0:T(8,128)(2,1)S(1)}, bf16[24,16,256]{2,1,0:T(8,128)(2,1)S(1)}, bf16[2,4,16,256]{3,2,1,0:T(8,128)(2,1)S(1)}) custom-call(f32[2,24,8,256]{3,2,1,0:T(8,128)S(1)} %get-tuple-element.28.refs_4_.now, f32[16,8,256]{2,1,0:T(8,128)S(1)} %get-tuple-element.29.sp, f32[2,16,8,256]{3,2,1,0:T(8,128)S(1)} %get-tuple-element.30.partial, ...), custom_call_target="tpu_custom_call" | custom-call | flops 9830400 | bytes 1638400 | tf_op jit(solution)/shard_map/pallas_call | solution.py:727
  11.7 0.1 collective-permute-start.3
  11.7 2.2 %collective-permute-start.2 = (bf16[24,16,256]{2,1,0:T(8,128)(2,1)S(1)}, bf16[24,16,256]{2,1,0:T(8,128)(2,1)S(1)}, u32[]{:S(2)}, u32[]{:S(2)}) collective-permute-start(bf16[24,16,256]{2,1,0:T(8,128)(2,1)S(1)} %get-tuple-element.38), channel_id=1, source_target_pairs={{0,15},{1,2},{2,1},{3,4},{4,3},{5,6},{6,5},{7,8},{8,7},{9,10},{10,... | collective-permute-start | bytes 589832 | tf_op jit(solution)/shard_map/ppermute | solution.py:645
  13.9 0.0 collective-permute-done.3.chip
  13.9 1.2 %collective-permute-start.6 = (bf16[2,2,8,16,256]{4,3,2,1,0:T(8,128)(2,1)S(1)}, bf16[2,2,8,16,256]{4,3,2,1,0:T(8,128)(2,1)S(1)}, u32[]{:S(2)}, u32[]{:S(2)}) collective-permute-start(bf16[2,2,8,16,256]{4,3,2,1,0:T(8,128)(2,1)S(1)} %collective-permute-done.3.chip), channel_id=1, source_target_pairs={{0,15},{1,2},{2,1},{3,4},{4,3},{5,6},{6,5},{7,8},{8,7},{9,10},{10,... | collective-permute-start | bytes 786440 | tf_op jit(solution)/shard_map/ppermute | solution.py:645
  15.1 7.1 %collective-permute-done.2.near = bf16[24,16,256]{2,1,0:T(8,128)(2,1)S(1)} collective-permute-done((bf16[24,16,256]{2,1,0:T(8,128)(2,1)S(1)}, bf16[24,16,256]{2,1,0:T(8,128)(2,1)S(1)}, u32[]{:S(2)}, u32[]{:S(2)}) %collective-permute-start.2) | collective-permute-done | bytes 196640 | tf_op jit(solution)/shard_map/ppermute | solution.py:645
  22.2 0.0 collective-permute-start.4
  22.2 0.5 %collective-permute-start.5 = (bf16[2,4,16,256]{3,2,1,0:T(8,128)(2,1)S(1)}, bf16[2,4,16,256]{3,2,1,0:T(8,128)(2,1)S(1)}, u32[]{:S(2)}, u32[]{:S(2)}) collective-permute-start(bf16[2,4,16,256]{3,2,1,0:T(8,128)(2,1)S(1)} %get-tuple-element.39.known), channel_id=1, source_target_pairs={{0,1},{1,0},{2,3},{3,2},{4,5},{5,4},{6,7},{7,6},{8,9},{9,8},{10,11... | collective-permute-start | bytes 196616 | tf_op jit(solution)/shard_map/ppermute | solution.py:645
  22.7 2.4 %shard_map.136 = (s32[8,16,256]{2,1,0:T(8,128)S(1)}, f32[25,4,8,128]{3,2,1,0:T(8,128)S(1)}, s32[8,128]{1,0:T(8,128)S(1)}, s32[8,128]{1,0:T(8,128)S(1)}) custom-call(s32[16,8,256]{2,1,0:T(8,128)} %bins_in.1, bf16[8,4,24]{2,1,0:T(4,128)(2,1)} %bitcast.3, s32[24]{0:T(128)} %lags_in.1), custom_call_target="tpu_custom_call" | custom-call | flops 32768 | bytes 262144 | tf_op jit(solution)/shard_map/pallas_call | solution.py:704
  25.1 1.3 %shard_map.140 = (f32[4,8,16,256]{3,2,1,0:T(8,128)S(1)}, f32[2,2,40,16,256]{4,3,2,1,0:T(8,128)S(1)}) custom-call(s32[8,128]{1,0:T(8,128)S(1)} %get-tuple-element.27.near_list, bf16[24,16,256]{2,1,0:T(8,128)(2,1)S(1)} %collective-permute-done.2.near, bf16[2,4,16,256]{3,2,1,0:T(8,128)(2,1)S(1)} %get-tuple-element.39.known, ...), custom_call_target="tpu_custom_call" | custom-call | flops 4718592 | bytes 655360 | tf_op jit(solution)/shard_map/pallas_call | solution.py:757
  26.4 0.0 collective-permute-done.5.hint
  26.4 0.0 collective-permute-done.4.relay
  26.4 0.8 %shard_map.141 = (f32[4,8,16,256]{3,2,1,0:T(8,128)S(1)}, f32[2,2,40,16,256]{4,3,2,1,0:T(8,128)S(1)}) custom-call(f32[4,8,16,256]{3,2,1,0:T(8,128)S(1)} %get-tuple-element.43.before_in, s32[8,128]{1,0:T(8,128)S(1)} %get-tuple-element.44.far_list, ...), custom_call_target="tpu_custom_call", output_to_operand_aliasing={{0}: (0, {}), {1}: (2, {})} | custom-call | flops 2359296 | bytes 655360 | tf_op jit(solution)/shard_map/pallas_call | solution.py:766
  27.2 0.0 collective-permute-done.6.far
  27.2 2.0 %shard_map.142 = (bf16[4,16,8,256]{3,2,1,0:T(8,128)(2,1)}, f32[2,2,40,16,256]{4,3,2,1,0:T(8,128)S(1)}) custom-call(f32[4,8,16,256]{3,2,1,0:T(8,128)S(1)} %get-tuple-element.46.before, s32[8,128]{1,0:T(8,128)S(1)} %get-tuple-element.44.far_list, f32[2,2,40,16,256]{4,3,2,1,0:T(8,128)S(1)} %get-tuple-element.47.window_in, ...), custom_call_target="tpu_custom_call", output_to_operand_aliasing={{1}: (2, {})} | custom-call | flops 2359296 | bytes 655360 | tf_op jit(solution)/shard_map/pallas_call | solution.py:778
Async XLA Ops:
  2.2 7.3 %collective-permute-start = (bf16[384,256]{1,0:T(8,128)(2,1)S(1)}, bf16[384,256]{1,0:T(8,128)(2,1)S(1)}, u32[]{:S(2)}, u32[]{:S(2)}) collective-permute-start(bf16[384,256]{1,0:T(8,128)(2,1)S(1)} %get-tuple-element.35), channel_id=1, source_target_pairs={{0,15},{1,2},{2,1},{3,4},{4,3},{5,6},{6,5},{7,8},{8,7},{9,10},{10,... | collective-permute-start | bytes 589832 | tf_op jit(solution)/shard_map/ppermute | solution.py:645
  4.1 5.5 %collective-permute-start.1 = (bf16[384,256]{1,0:T(8,128)(2,1)S(1)}, bf16[384,256]{1,0:T(8,128)(2,1)S(1)}, u32[]{:S(2)}, u32[]{:S(2)}) collective-permute-start(bf16[384,256]{1,0:T(8,128)(2,1)S(1)} %get-tuple-element.36), channel_id=1, source_target_pairs={{0,1},{1,0},{2,3},{3,2},{4,5},{5,4},{6,7},{7,6},{8,9},{9,8},{10,11... | collective-permute-start | bytes 589832 | tf_op jit(solution)/shard_map/ppermute | solution.py:645
  11.7 2.2 %collective-permute-start.3 = (bf16[2,2,8,16,256]{4,3,2,1,0:T(8,128)(2,1)S(1)}, bf16[2,2,8,16,256]{4,3,2,1,0:T(8,128)(2,1)S(1)}, u32[]{:S(2)}, u32[]{:S(2)}) collective-permute-start(bf16[2,2,8,16,256]{4,3,2,1,0:T(8,128)(2,1)S(1)} %get-tuple-element.40.own), channel_id=1, source_target_pairs={{0,1},{1,0},{2,3},{3,2},{4,5},{5,4},{6,7},{7,6},{8,9},{9,8},{10,11... | collective-permute-start | bytes 786440 | tf_op jit(solution)/shard_map/ppermute | solution.py:645
  11.7 10.4 %collective-permute-start.2 = (bf16[24,16,256]{2,1,0:T(8,128)(2,1)S(1)}, bf16[24,16,256]{2,1,0:T(8,128)(2,1)S(1)}, u32[]{:S(2)}, u32[]{:S(2)}) collective-permute-start(bf16[24,16,256]{2,1,0:T(8,128)(2,1)S(1)} %get-tuple-element.38), channel_id=1, source_target_pairs={{0,15},{1,2},{2,1},{3,4},{4,3},{5,6},{6,5},{7,8},{8,7},{9,10},{10,... | collective-permute-start | bytes 589832 | tf_op jit(solution)/shard_map/ppermute | solution.py:645
  13.9 13.3 %collective-permute-start.6 = (bf16[2,2,8,16,256]{4,3,2,1,0:T(8,128)(2,1)S(1)}, bf16[2,2,8,16,256]{4,3,2,1,0:T(8,128)(2,1)S(1)}, u32[]{:S(2)}, u32[]{:S(2)}) collective-permute-start(bf16[2,2,8,16,256]{4,3,2,1,0:T(8,128)(2,1)S(1)} %collective-permute-done.3.chip), channel_id=1, source_target_pairs={{0,15},{1,2},{2,1},{3,4},{4,3},{5,6},{6,5},{7,8},{8,7},{9,10},{10,... | collective-permute-start | bytes 786440 | tf_op jit(solution)/shard_map/ppermute | solution.py:645
  22.2 4.3 %collective-permute-start.4 = (bf16[24,16,256]{2,1,0:T(8,128)(2,1)S(1)}, bf16[24,16,256]{2,1,0:T(8,128)(2,1)S(1)}, u32[]{:S(2)}, u32[]{:S(2)}) collective-permute-start(bf16[24,16,256]{2,1,0:T(8,128)(2,1)S(1)} %collective-permute-done.2.near), channel_id=1, source_target_pairs={{0,1},{1,0},{2,3},{3,2},{4,5},{5,4},{6,7},{7,6},{8,9},{9,8},{10,11... | collective-permute-start | bytes 589832 | tf_op jit(solution)/shard_map/ppermute | solution.py:645
  22.2 4.2 %collective-permute-start.5 = (bf16[2,4,16,256]{3,2,1,0:T(8,128)(2,1)S(1)}, bf16[2,4,16,256]{3,2,1,0:T(8,128)(2,1)S(1)}, u32[]{:S(2)}, u32[]{:S(2)}) collective-permute-start(bf16[2,4,16,256]{3,2,1,0:T(8,128)(2,1)S(1)} %get-tuple-element.39.known), channel_id=1, source_target_pairs={{0,1},{1,0},{2,3},{3,2},{4,5},{5,4},{6,7},{7,6},{8,9},{9,8},{10,11... | collective-permute-start | bytes 196616 | tf_op jit(solution)/shard_map/ppermute | solution.py:645

commit v5 on v4

--- a/solution.py
+++ b/solution.py
@@ -414,7 +414,7 @@
                     )
         return c
 
-    lax.fori_loop(0, depth // 2, flat, 0, unroll=2)
+    lax.fori_loop(0, depth // 2, flat, 0, unroll=4)
 
     def deep(z, c):
         for m in range(2):
@@ -422,7 +422,7 @@
             later_edge[m, z] = edge_base[m, z] + edge_tilt[z] * depth_first(edge_slope.at[m], z)
         return c
 
-    lax.fori_loop(0, depth, deep, 0, unroll=4)
+    lax.fori_loop(0, depth, deep, 0, unroll=8)
     for m in range(2):
         later[m, REACH] = later[m, REACH] + inj[0, m]
         later_edge[m, 0] = later_edge[m, 0] + inj[1, m]
@@ -442,7 +442,7 @@
                 turned[2, m, p, pl.ds(z, rows, stride=depth), :] = later_edge[m, z, :, lanes]
         return c
 
-    lax.fori_loop(0, depth, flat_later, 0, unroll=4)
+    lax.fori_loop(0, depth, flat_later, 0, unroll=8)
 
     def deep_later(z, c):
         surface = jnp.where(z == 0, 1.0, 0.0)
@@ -457,7 +457,7 @@
                 turned[1, m, p, pl.ds(z, rows, stride=depth), :] = value[:, lanes]
         return c
 
-    lax.fori_loop(0, depth, deep_later, 0, unroll=4)
+    lax.fori_loop(0, depth, deep_later, 0, unroll=8)
     kept = jnp.where(odd, 0, half)
     for m in range(2):
         for p, lanes in enumerate(parts):
@@ -473,7 +473,7 @@
                 known[m, y, :, lanes] = turned[2, m, p, plane, :].astype(BF16)
 
 
-PAIR = 2
+PAIR = 4
 
 
 def add_lags(window, table, ids, picks, groups, rows, spots, sums):

time: 29.5 us -> 29.1 us (0.986)
  Pallas kernels: 12.5 us -> 12.1 us
where the time goes in v5:
time: 29.1 us; the launch traced here: 28.9 us
  Pallas kernels  12.1 us (42%)
  waiting for transfers between devices  10.9 us (37%)
  starting transfers between devices  5.76 us (20%)
    ppermute x7, waiting for transfers between devices, moved(): return lax.ppermute(block, 'gy', route)  10.9 us
    ppermute x7, starting transfers between devices, moved(): return lax.ppermute(block, 'gy', route)  5.76 us
    pallas_call x1, Pallas kernels, per_device(): call(table_kernel, [jax.ShapeDtypeStruct((rows, depth, width), jnp.int32)...  2.41 us
    pallas_call x1, Pallas kernels, per_device(): call(pack_kernel, [pack_shape, pack_shape, jax.ShapeDtypeStruct((2, tall,...  2.24 us
    pallas_call x1, Pallas kernels, per_device(): call(far_image_kernel, [jax.ShapeDtypeStruct((angles, depth, rows, width)...  2.02 us
    pallas_call x1, Pallas kernels, per_device(): call(step_kernel, [jax.ShapeDtypeStruct((STEPS, 2, rows, depth, width), B...  1.85 us
    pallas_call x1, Pallas kernels, per_device(): call(functools.partial(inject_kernel, size * rows), [jax.ShapeDtypeStruct...  1.64 us
    pallas_call x1, Pallas kernels, per_device(): call(near_image_kernel, [jax.ShapeDtypeStruct((angles, rows, depth, width...  1.31 us
  transfers between devices with their start and end apart: 7, of which 2 were waited for; matrix products, arithmetic and copies ran while one was open for 0% of the time, Pallas kernels for 21%

profile of v5, /device:TPU:25, one launch (start us, length us, event | category | flops | bytes accessed | tf_op | source)
XLA Modules:
  0.0 28.9 jit_solution(7453726746202570373)
XLA Ops:
  0.0 2.2 %shard_map.137 = (bf16[384,256]{1,0:T(8,128)(2,1)S(1)}, bf16[384,256]{1,0:T(8,128)(2,1)S(1)}, f32[2,24,8,256]{3,2,1,0:T(8,128)S(1)}, f32[16,8,256]{2,1,0:T(8,128...) custom-call(f32[16,8,256]{2,1,0:T(8,128)} %refs_0_.1, ...), custom_call_target="tpu_custom_call" | custom-call | flops 6553600 | bytes 1310720 | tf_op jit(solution)/shard_map/pallas_call | solution.py:654
  2.2 1.9 %collective-permute-start = (bf16[384,256]{1,0:T(8,128)(2,1)S(1)}, bf16[384,256]{1,0:T(8,128)(2,1)S(1)}, u32[]{:S(2)}, u32[]{:S(2)}) collective-permute-start(bf16[384,256]{1,0:T(8,128)(2,1)S(1)} %get-tuple-element.35), channel_id=1, source_target_pairs={{0,15},{1,2},{2,1},{3,4},{4,3},{5,6},{6,5},{7,8},{8,7},{9,10},{10,... | collective-permute-start | bytes 589832 | tf_op jit(solution)/shard_map/ppermute | solution.py:645
  4.1 0.0 collective-permute-start.1
  4.1 1.6 %shard_map.138 = (f32[3,2,8,256]{3,2,1,0:T(8,128)S(1)}, f32[2,16,8,256]{3,2,1,0:T(8,128)S(1)}, f32[2,24,8,256]{3,2,1,0:T(8,128)S(1)}) custom-call(s32[1,2048]{1,0:T(1,128)} %bitcast.2, f32[2,2048]{1,0:T(2,128)} %refs_1_.3, s32[8]{0:T(128)} %refs_2_.3, f32[2,8]{1,0:T(2,128)} %refs_3_.3, f32[2,24,8,256]{3,2,1,0:T(8,128)S(1)} %get-tuple-element.28.refs_4_.now), custom_call_target="tpu_custom_call" | custom-call | flops 50331648 | bytes 262144 | tf_op jit(solution)/shard_map/pallas_call | solution.py:679
  5.8 3.8 %collective-permute-done.px = bf16[384,256]{1,0:T(8,128)(2,1)S(1)} collective-permute-done((bf16[384,256]{1,0:T(8,128)(2,1)S(1)}, bf16[384,256]{1,0:T(8,128)(2,1)S(1)}, u32[]{:S(2)}, u32[]{:S(2)}) %collective-permute-start) | collective-permute-done | bytes 196640 | tf_op jit(solution)/shard_map/ppermute | solution.py:645
  9.6 0.0 collective-permute-done.1.ps
  9.6 1.9 %shard_map.139 = (bf16[2,2,8,16,256]{4,3,2,1,0:T(8,128)(2,1)S(1)}, bf16[24,16,256]{2,1,0:T(8,128)(2,1)S(1)}, bf16[2,4,16,256]{3,2,1,0:T(8,128)(2,1)S(1)}) custom-call(f32[2,24,8,256]{3,2,1,0:T(8,128)S(1)} %get-tuple-element.28.refs_4_.now, f32[16,8,256]{2,1,0:T(8,128)S(1)} %get-tuple-element.29.sp, f32[2,16,8,256]{3,2,1,0:T(8,128)S(1)} %get-tuple-element.30.partial, ...), custom_call_target="tpu_custom_call" | custom-call | flops 9830400 | bytes 1638400 | tf_op jit(solution)/shard_map/pallas_call | solution.py:727
  11.4 0.1 collective-permute-start.3
  11.5 2.2 %collective-permute-start.2 = (bf16[24,16,256]{2,1,0:T(8,128)(2,1)S(1)}, bf16[24,16,256]{2,1,0:T(8,128)(2,1)S(1)}, u32[]{:S(2)}, u32[]{:S(2)}) collective-permute-start(bf16[24,16,256]{2,1,0:T(8,128)(2,1)S(1)} %get-tuple-element.38), channel_id=1, source_target_pairs={{0,15},{1,2},{2,1},{3,4},{4,3},{5,6},{6,5},{7,8},{8,7},{9,10},{10,... | collective-permute-start | bytes 589832 | tf_op jit(solution)/shard_map/ppermute | solution.py:645
  13.7 0.0 collective-permute-done.3.chip
  13.7 1.2 %collective-permute-start.6 = (bf16[2,2,8,16,256]{4,3,2,1,0:T(8,128)(2,1)S(1)}, bf16[2,2,8,16,256]{4,3,2,1,0:T(8,128)(2,1)S(1)}, u32[]{:S(2)}, u32[]{:S(2)}) collective-permute-start(bf16[2,2,8,16,256]{4,3,2,1,0:T(8,128)(2,1)S(1)} %collective-permute-done.3.chip), channel_id=1, source_target_pairs={{0,15},{1,2},{2,1},{3,4},{4,3},{5,6},{6,5},{7,8},{8,7},{9,10},{10,... | collective-permute-start | bytes 786440 | tf_op jit(solution)/shard_map/ppermute | solution.py:645
  14.8 7.1 %collective-permute-done.2.near = bf16[24,16,256]{2,1,0:T(8,128)(2,1)S(1)} collective-permute-done((bf16[24,16,256]{2,1,0:T(8,128)(2,1)S(1)}, bf16[24,16,256]{2,1,0:T(8,128)(2,1)S(1)}, u32[]{:S(2)}, u32[]{:S(2)}) %collective-permute-start.2) | collective-permute-done | bytes 196640 | tf_op jit(solution)/shard_map/ppermute | solution.py:645
  21.9 0.0 collective-permute-start.4
  21.9 0.5 %collective-permute-start.5 = (bf16[2,4,16,256]{3,2,1,0:T(8,128)(2,1)S(1)}, bf16[2,4,16,256]{3,2,1,0:T(8,128)(2,1)S(1)}, u32[]{:S(2)}, u32[]{:S(2)}) collective-permute-start(bf16[2,4,16,256]{3,2,1,0:T(8,128)(2,1)S(1)} %get-tuple-element.39.known), channel_id=1, source_target_pairs={{0,1},{1,0},{2,3},{3,2},{4,5},{5,4},{6,7},{7,6},{8,9},{9,8},{10,11... | collective-permute-start | bytes 196616 | tf_op jit(solution)/shard_map/ppermute | solution.py:645
  22.4 2.4 %shard_map.136 = (s32[8,16,256]{2,1,0:T(8,128)S(1)}, f32[25,4,8,128]{3,2,1,0:T(8,128)S(1)}, s32[8,128]{1,0:T(8,128)S(1)}, s32[8,128]{1,0:T(8,128)S(1)}) custom-call(s32[16,8,256]{2,1,0:T(8,128)} %bins_in.1, bf16[8,4,24]{2,1,0:T(4,128)(2,1)} %bitcast.3, s32[24]{0:T(128)} %lags_in.1), custom_call_target="tpu_custom_call" | custom-call | flops 32768 | bytes 262144 | tf_op jit(solution)/shard_map/pallas_call | solution.py:704
  24.9 1.3 %shard_map.140 = (f32[4,8,16,256]{3,2,1,0:T(8,128)S(1)}, f32[2,2,40,16,256]{4,3,2,1,0:T(8,128)S(1)}) custom-call(s32[8,128]{1,0:T(8,128)S(1)} %get-tuple-element.27.near_list, bf16[24,16,256]{2,1,0:T(8,128)(2,1)S(1)} %collective-permute-done.2.near, bf16[2,4,16,256]{3,2,1,0:T(8,128)(2,1)S(1)} %get-tuple-element.39.known, ...), custom_call_target="tpu_custom_call" | custom-call | flops 4718592 | bytes 655360 | tf_op jit(solution)/shard_map/pallas_call | solution.py:757
  26.2 0.0 collective-permute-done.5.hint
  26.2 0.0 collective-permute-done.4.relay
  26.2 0.6 %shard_map.141 = (f32[4,8,16,256]{3,2,1,0:T(8,128)S(1)}, f32[2,2,40,16,256]{4,3,2,1,0:T(8,128)S(1)}) custom-call(f32[4,8,16,256]{3,2,1,0:T(8,128)S(1)} %get-tuple-element.43.before_in, s32[8,128]{1,0:T(8,128)S(1)} %get-tuple-element.44.far_list, ...), custom_call_target="tpu_custom_call", output_to_operand_aliasing={{0}: (0, {}), {1}: (2, {})} | custom-call | flops 2359296 | bytes 655360 | tf_op jit(solution)/shard_map/pallas_call | solution.py:766
  26.8 0.0 collective-permute-done.6.far
  26.8 2.0 %shard_map.142 = (bf16[4,16,8,256]{3,2,1,0:T(8,128)(2,1)}, f32[2,2,40,16,256]{4,3,2,1,0:T(8,128)S(1)}) custom-call(f32[4,8,16,256]{3,2,1,0:T(8,128)S(1)} %get-tuple-element.46.before, s32[8,128]{1,0:T(8,128)S(1)} %get-tuple-element.44.far_list, f32[2,2,40,16,256]{4,3,2,1,0:T(8,128)S(1)} %get-tuple-element.47.window_in, ...), custom_call_target="tpu_custom_call", output_to_operand_aliasing={{1}: (2, {})} | custom-call | flops 2359296 | bytes 655360 | tf_op jit(solution)/shard_map/pallas_call | solution.py:778
Async XLA Ops:
  2.2 7.3 %collective-permute-start = (bf16[384,256]{1,0:T(8,128)(2,1)S(1)}, bf16[384,256]{1,0:T(8,128)(2,1)S(1)}, u32[]{:S(2)}, u32[]{:S(2)}) collective-permute-start(bf16[384,256]{1,0:T(8,128)(2,1)S(1)} %get-tuple-element.35), channel_id=1, source_target_pairs={{0,15},{1,2},{2,1},{3,4},{4,3},{5,6},{6,5},{7,8},{8,7},{9,10},{10,... | collective-permute-start | bytes 589832 | tf_op jit(solution)/shard_map/ppermute | solution.py:645
  4.1 5.5 %collective-permute-start.1 = (bf16[384,256]{1,0:T(8,128)(2,1)S(1)}, bf16[384,256]{1,0:T(8,128)(2,1)S(1)}, u32[]{:S(2)}, u32[]{:S(2)}) collective-permute-start(bf16[384,256]{1,0:T(8,128)(2,1)S(1)} %get-tuple-element.36), channel_id=1, source_target_pairs={{0,1},{1,0},{2,3},{3,2},{4,5},{5,4},{6,7},{7,6},{8,9},{9,8},{10,11... | collective-permute-start | bytes 589832 | tf_op jit(solution)/shard_map/ppermute | solution.py:645
  11.4 2.2 %collective-permute-start.3 = (bf16[2,2,8,16,256]{4,3,2,1,0:T(8,128)(2,1)S(1)}, bf16[2,2,8,16,256]{4,3,2,1,0:T(8,128)(2,1)S(1)}, u32[]{:S(2)}, u32[]{:S(2)}) collective-permute-start(bf16[2,2,8,16,256]{4,3,2,1,0:T(8,128)(2,1)S(1)} %get-tuple-element.40.own), channel_id=1, source_target_pairs={{0,1},{1,0},{2,3},{3,2},{4,5},{5,4},{6,7},{7,6},{8,9},{9,8},{10,11... | collective-permute-start | bytes 786440 | tf_op jit(solution)/shard_map/ppermute | solution.py:645
  11.5 10.4 %collective-permute-start.2 = (bf16[24,16,256]{2,1,0:T(8,128)(2,1)S(1)}, bf16[24,16,256]{2,1,0:T(8,128)(2,1)S(1)}, u32[]{:S(2)}, u32[]{:S(2)}) collective-permute-start(bf16[24,16,256]{2,1,0:T(8,128)(2,1)S(1)} %get-tuple-element.38), channel_id=1, source_target_pairs={{0,15},{1,2},{2,1},{3,4},{4,3},{5,6},{6,5},{7,8},{8,7},{9,10},{10,... | collective-permute-start | bytes 589832 | tf_op jit(solution)/shard_map/ppermute | solution.py:645
  13.7 13.2 %collective-permute-start.6 = (bf16[2,2,8,16,256]{4,3,2,1,0:T(8,128)(2,1)S(1)}, bf16[2,2,8,16,256]{4,3,2,1,0:T(8,128)(2,1)S(1)}, u32[]{:S(2)}, u32[]{:S(2)}) collective-permute-start(bf16[2,2,8,16,256]{4,3,2,1,0:T(8,128)(2,1)S(1)} %collective-permute-done.3.chip), channel_id=1, source_target_pairs={{0,15},{1,2},{2,1},{3,4},{4,3},{5,6},{6,5},{7,8},{8,7},{9,10},{10,... | collective-permute-start | bytes 786440 | tf_op jit(solution)/shard_map/ppermute | solution.py:645
  21.9 4.3 %collective-permute-start.4 = (bf16[24,16,256]{2,1,0:T(8,128)(2,1)S(1)}, bf16[24,16,256]{2,1,0:T(8,128)(2,1)S(1)}, u32[]{:S(2)}, u32[]{:S(2)}) collective-permute-start(bf16[24,16,256]{2,1,0:T(8,128)(2,1)S(1)} %collective-permute-done.2.near), channel_id=1, source_target_pairs={{0,1},{1,0},{2,3},{3,2},{4,5},{5,4},{6,7},{7,6},{8,9},{9,8},{10,11... | collective-permute-start | bytes 589832 | tf_op jit(solution)/shard_map/ppermute | solution.py:645
  21.9 4.2 %collective-permute-start.5 = (bf16[2,4,16,256]{3,2,1,0:T(8,128)(2,1)S(1)}, bf16[2,4,16,256]{3,2,1,0:T(8,128)(2,1)S(1)}, u32[]{:S(2)}, u32[]{:S(2)}) collective-permute-start(bf16[2,4,16,256]{3,2,1,0:T(8,128)(2,1)S(1)} %get-tuple-element.39.known), channel_id=1, source_target_pairs={{0,1},{1,0},{2,3},{3,2},{4,5},{5,4},{6,7},{7,6},{8,9},{9,8},{10,11... | collective-permute-start | bytes 196616 | tf_op jit(solution)/shard_map/ppermute | solution.py:645
